TPU v7x, 128 devices: a whole 4x4x4 slice. The times are simulated.
128 devices in a mesh: freq: 4 (over x_hi, core), sky: 32 (over x_lo, y, z).
Axes of the slice: x: 4 (x_hi: 2, x_lo: 2; x = x_hi * 2 + x_lo), y: 4, z: 4, core: 2. Of those that a mesh axis runs over, the one named last changes fastest.
Arguments:
- sky_cube: bfloat16 [16, 1024, 1024], P('freq', 'sky'), may hold values from -6 to 6
- half_width: int32 [16], P('freq'), may hold values from 2 to 12, as said below
- conv_weight: bfloat16 [16, 27], replicated, may hold values from -0.3125 to 0.3125
- out_cotangent: bfloat16 [16, 16, 1024, 1024], P(None, 'freq', 'sky'), may hold values from -6 to 6
Outputs:
- sky_grad: float32 [16, 1024, 1024], P('freq', 'sky')
- kernel_grad: float32 [16, 27], replicated
Inputs may be any that keep to these rules, and one draw needn't show every extreme that they name: half_width[f] differs by at most one from 2 + floor((10) (15 - f) / 15); the first frequency has exactly 12 and the last exactly 2.
All inputs are finite; a program needn't handle non-finite values.
Results may differ from a plain program's by a relative error of at most 0.0033.
Values may be sent and summed in bfloat16 or wider, within the bound.
No kernel may reach another device: no remote copies, remote signals or barrier semaphores. Data moves between devices by JAX's collectives and lax.ppermute only.
A program may use at most 128 MiB of HBM per device.

v0:
```python
import math

import jax
import jax.numpy as jnp
from jax import lax
from jax.experimental import pallas as pl
from jax.experimental.pallas import tpu as pltpu
from jax.sharding import PartitionSpec as P

MAXH = 12
HALF = 16
F32 = jnp.float32
BF16 = jnp.bfloat16
VMEM_LIMIT = 48 * 1024 * 1024


def params():
    return pltpu.CompilerParams(vmem_limit_bytes=VMEM_LIMIT)


def iota(shape, dim):
    return lax.broadcasted_iota(jnp.int32, shape, dim)


def dot(a, b):
    return jnp.dot(a, b, preferred_element_type=F32)


def split(x):
    hi = x.astype(BF16)
    return hi, (x - hi.astype(F32)).astype(BF16)


def taps_at(offsets, width):
    def profile(d):
        w = jnp.full(d.shape, width, jnp.int32)
        wf = w.astype(F32)
        df = d.astype(F32)
        return jnp.where(jnp.abs(d) <= w, jnp.exp(-2.0 * (df * df) / (wf * wf)), 0.0)

    line = profile(iota((8, 128), 1) - 64)
    norm = jnp.sqrt(jnp.sum(line * line, axis=1, keepdims=True))[:1]
    return profile(offsets) / norm


def column_matrices(width):
    band = taps_at(iota((160, 128), 0) - 16 - iota((160, 128), 1), width)
    left = jnp.concatenate([jnp.zeros((112, 128), F32), band, jnp.zeros((240, 128), F32)], axis=0)
    right = jnp.concatenate([jnp.zeros((240, 128), F32), band, jnp.zeros((112, 128), F32)], axis=0)
    return split(jnp.concatenate([left, right], axis=1))


def blur_columns(rows, width):
    n = rows.shape[0]
    hi, lo = column_matrices(width)
    edge = jnp.zeros((n, 128), BF16)
    padded = jnp.concatenate([edge, rows, edge], axis=1)
    stacked = jnp.concatenate([padded[:, 256 * j : 256 * j + 512] for j in range(4)], axis=0)
    out = dot(stacked, hi) + dot(stacked, lo)
    return jnp.concatenate([out[n * j : n * j + n] for j in range(4)], axis=1)


def blur_rows(source, count, base, width):
    n = source.shape[0]
    matrix = taps_at(iota((count, n), 1) - iota((count, n), 0) - base, width)
    m_hi, m_lo = split(matrix)
    hi, lo = split(source)
    return dot(m_hi, hi) + dot(m_hi, lo) + dot(m_lo, hi)


def shift_cols(x, offset):
    if offset == 0:
        return x
    length = x.shape[-1]
    col = iota(x.shape, x.ndim - 1)
    if offset > 0:
        return jnp.where(col < length - 1, pltpu.roll(x, length - 1, x.ndim - 1), 0.0)
    return jnp.where(col > 0, pltpu.roll(x, 1, x.ndim - 1), 0.0)


def back_kernel(weight_ref, cot_ref, out_ref, mat_ref, acc_ref):
    f = pl.program_id(0)

    @pl.when(f == 0)
    def _():
        expand = (iota((16, 512), 1) // 32 == iota((16, 512), 0)).astype(BF16)
        w = lax.dot_general(weight_ref[...], expand, (((0,), (0,)), ((), ())), preferred_element_type=F32)
        diff = iota((40, 512), 0) - iota((40, 512), 1) % 32
        blocks = []
        for a in range(3):
            for e in range(3):
                block = jnp.zeros((40, 512), F32)
                for b in range(3):
                    row = w[9 * a + 3 * b + e : 9 * a + 3 * b + e + 1, :]
                    block = jnp.where(diff == b, row, block)
                blocks.append(block)
        mat_ref[...] = jnp.concatenate(blocks, axis=0).astype(BF16)
        acc_ref[...] = jnp.zeros_like(acc_ref)

    cot = cot_ref[...].reshape(512, 1024)
    terms = dot(mat_ref[...], cot)
    for a in range(3):
        acc_ref[pl.ds(f + a, 1)] += terms[120 * a : 120 * a + 120][None]

    @pl.when(f == pl.num_programs(0) - 1)
    def _():
        for p in range(6):
            full = acc_ref[p]
            out_ref[p] = shift_cols(full[0:40], 1) + full[40:80] + shift_cols(full[80:120], -1)


def back_project(conv_weight, out_cotangent):
    return pl.pallas_call(
        back_kernel,
        grid=(4,),
        out_shape=jax.ShapeDtypeStruct((6, 40, 1024), F32),
        in_specs=[
            pl.BlockSpec((16, 27), lambda f: (0, 0)),
            pl.BlockSpec((16, 1, 32, 1024), lambda f: (0, f, 0, 0)),
        ],
        out_specs=pl.BlockSpec((6, 40, 1024), lambda f: (0, 0, 0)),
        scratch_shapes=[pltpu.VMEM((360, 512), BF16), pltpu.VMEM((6, 120, 1024), F32)],
        compiler_params=params(),
        cost_estimate=pl.CostEstimate(flops=3 * 10**9, bytes_accessed=6 * 2**20, transcendentals=0),
        name="back_project",
    )(conv_weight, out_cotangent)


def beam_kernel(where_ref, width_ref, sky_ref, a_ref, b_ref, beam_ref):
    even = where_ref[0] % 2 == 0
    row = iota((48, 1024), 0)
    first = jnp.where(where_ref[0] == 0, 1, 0)
    last = jnp.where(where_ref[0] == 31, 33, 34)
    keep = (row >= first) & (row < last)
    for f in range(4):
        width = width_ref[f]
        ra, rb = a_ref[f], b_ref[f]
        above = jnp.where(even, rb, ra)
        below = jnp.where(even, ra, rb)
        rows = jnp.concatenate([above, sky_ref[f], below], axis=0)
        smooth = blur_columns(rows, width)
        beam = jnp.where(keep, blur_rows(smooth, 48, 15, width), 0.0)
        beam_ref[f] = beam.astype(BF16)


def smem():
    return pl.BlockSpec(memory_space=pltpu.SMEM)


def vmem():
    return pl.BlockSpec(memory_space=pltpu.VMEM)


def beam_of(place, half_width, sky_cube, from_a, from_b):
    return pl.pallas_call(
        beam_kernel,
        out_shape=jax.ShapeDtypeStruct((4, 48, 1024), BF16),
        in_specs=[smem(), smem(), vmem(), vmem(), vmem()],
        out_specs=vmem(),
        compiler_params=params(),
        cost_estimate=pl.CostEstimate(flops=2 * 10**9, bytes_accessed=2**20, transcendentals=10**5),
        name="beam",
    )(place, half_width, sky_cube, from_a, from_b)


def three_shifts(beam):
    wide = beam.astype(F32)
    return jnp.concatenate([shift_cols(wide, e - 1).astype(BF16) for e in range(3)], axis=0)


def pick_taps(gram, first_group):
    n = gram.shape[1]
    shape = (512, n)
    diff = iota(shape, 1) % 48 - iota(shape, 0) % 32
    total = jnp.zeros((16, 128), F32)
    for b in range(3):
        part = jnp.where(diff == b, gram, 0.0).reshape(16, 32, n).sum(axis=1)
        group = iota((n, 128), 0) // 48 + first_group
        tap = 9 * (group // 3) + 3 * b + group % 3
        chosen = (iota((n, 128), 1) % 32 == tap).astype(F32)
        total = total + jnp.dot(part, chosen, preferred_element_type=F32, precision=lax.Precision.HIGHEST)
    return total


def contract(a, b):
    return lax.dot_general(a, b, (((1,), (1,)), ((), ())), preferred_element_type=F32)


def inner_kernel(beam_ref, cot_ref, out_ref, shift_ref, gram_ref):
    f = pl.program_id(0)

    @pl.when(f == 0)
    def _():
        gram_ref[...] = jnp.zeros_like(gram_ref)
        shift_ref[pl.ds(0, 144)] = jnp.zeros((144, 1024), BF16)
        shift_ref[pl.ds(720, 144)] = jnp.zeros((144, 1024), BF16)
        for p in range(4):
            shift_ref[pl.ds(144 * (p + 1), 144)] = three_shifts(beam_ref[p])

    cot = cot_ref[...].reshape(512, 1024)
    start = pl.multiple_of(f * 144, 16)
    gram_ref[...] += contract(cot, shift_ref[pl.ds(start, 432)])

    @pl.when(f == pl.num_programs(0) - 1)
    def _():
        out_ref[...] = pick_taps(gram_ref[...], 0)


def inner_terms(beam, out_cotangent):
    return pl.pallas_call(
        inner_kernel,
        grid=(4,),
        out_shape=jax.ShapeDtypeStruct((16, 128), F32),
        in_specs=[
            pl.BlockSpec((4, 48, 1024), lambda f: (0, 0, 0)),
            pl.BlockSpec((16, 1, 32, 1024), lambda f: (0, f, 0, 0)),
        ],
        out_specs=pl.BlockSpec((16, 128), lambda f: (0, 0)),
        scratch_shapes=[pltpu.VMEM((864, 1024), BF16), pltpu.VMEM((512, 432), F32)],
        compiler_params=params(),
        cost_estimate=pl.CostEstimate(flops=3 * 10**9, bytes_accessed=6 * 2**20, transcendentals=0),
        name="inner_terms",
    )(beam, out_cotangent)


def outer_kernel(where_ref, inner_ref, core_ref, far_ref, first_ref, last_ref, out_ref):
    even = where_ref[1] % 2 == 0
    core, far = core_ref[...], far_ref[...]
    before = jnp.where(even, far, core)
    after = jnp.where(even, core, far)
    low = contract(first_ref[...].reshape(512, 1024), three_shifts(before))
    high = contract(last_ref[...].reshape(512, 1024), three_shifts(after))
    total = inner_ref[...] + pick_taps(low, 0) + pick_taps(high, 6)
    placed = jnp.where(iota((16, 128), 1) // 32 == iota((16, 128), 0) % 4, total, 0.0)
    packed = placed.reshape(4, 4, 128).sum(axis=1)
    out_ref[...] = jnp.broadcast_to(packed[None], out_ref.shape)


def outer_terms(place, inner, from_core, from_far, out_cotangent, copies):
    plane = (16, 1, 32, 1024)
    whole = lambda i: (0, 0)
    return pl.pallas_call(
        outer_kernel,
        grid=(1,),
        out_shape=jax.ShapeDtypeStruct((copies, 4, 128), F32),
        in_specs=[
            smem(),
            pl.BlockSpec((16, 128), whole),
            pl.BlockSpec((48, 1024), whole),
            pl.BlockSpec((48, 1024), whole),
            pl.BlockSpec(plane, lambda i: (0, 0, 0, 0)),
            pl.BlockSpec(plane, lambda i: (0, 3, 0, 0)),
        ],
        out_specs=pl.BlockSpec((copies, 4, 128), lambda i: (0, 0, 0)),
        compiler_params=params(),
        cost_estimate=pl.CostEstimate(flops=5 * 10**8, bytes_accessed=3 * 2**20, transcendentals=0),
        name="outer_terms",
    )(place, inner, from_core, from_far, out_cotangent, out_cotangent)


def spread_kernel(where_ref, width_ref, grad_ref, core_ref, far_ref, own_ref, up_ref, down_ref):
    even = where_ref[1] % 2 == 0
    core, far = core_ref[...], far_ref[...]
    row = iota((40, 1024), 0)
    first = jnp.where(where_ref[0] == 0, 1, 0)
    last = jnp.where(where_ref[0] == 31, 33, 34)
    keep = (row >= first) & (row < last)
    shared = (row < 2) | (row >= 32)
    for f in range(4):
        width = width_ref[f]
        grad = grad_ref[f + 1]
        if f == 0:
            grad = grad + jnp.where(even, far, core)
        if f == 3:
            grad = grad + jnp.where(even, core, far)
        grad = jnp.where(keep, grad, 0.0)
        hi = grad.astype(BF16).astype(F32)
        lo = jnp.where(shared, grad - hi, 0.0)
        both = jnp.concatenate([hi, lo], axis=0).astype(BF16)
        smooth = blur_columns(both, width)
        out = blur_rows(smooth[:40] + smooth[40:], 64, -15, width)
        up_ref[f] = out[:16]
        own_ref[f] = out[16:48]
        down_ref[f] = out[48:]


def spread(place, half_width, grad, from_core, from_far):
    return pl.pallas_call(
        spread_kernel,
        out_shape=(
            jax.ShapeDtypeStruct((4, 32, 1024), F32),
            jax.ShapeDtypeStruct((4, 16, 1024), F32),
            jax.ShapeDtypeStruct((4, 16, 1024), F32),
        ),
        in_specs=[smem(), smem(), vmem(), vmem(), vmem()],
        out_specs=(vmem(), vmem(), vmem()),
        compiler_params=params(),
        cost_estimate=pl.CostEstimate(flops=3 * 10**9, bytes_accessed=3 * 2**20, transcendentals=10**5),
        name="spread",
    )(place, half_width, grad, from_core, from_far)


def final_kernel(scale, where_ref, own_ref, a_ref, b_ref, terms_ref, sky_ref, grad_ref):
    even = where_ref[0] % 2 == 0
    for f in range(4):
        ra, rb = a_ref[f], b_ref[f]
        sky_ref[f, :HALF] = own_ref[f, :HALF] + jnp.where(even, rb, ra)
        sky_ref[f, HALF:] = own_ref[f, HALF:] + jnp.where(even, ra, rb)
    packed = jnp.sum(terms_ref[...], axis=0) * scale
    rows = jnp.broadcast_to(packed[:, None, :], (4, 4, 128)).reshape(16, 128)
    placed = jnp.where(iota((16, 128), 1) // 32 == iota((16, 128), 0) % 4, rows, 0.0)
    fold = (iota((128, 128), 0) % 32 == iota((128, 128), 1)).astype(F32)
    out = jnp.dot(placed, fold, preferred_element_type=F32, precision=lax.Precision.HIGHEST)
    grad_ref[...] = out[:, :27]


def finish(scale, place, own, from_a, from_b, terms):
    def body(*refs):
        final_kernel(scale, *refs)

    return pl.pallas_call(
        body,
        out_shape=(jax.ShapeDtypeStruct((4, 32, 1024), F32), jax.ShapeDtypeStruct((16, 27), F32)),
        in_specs=[smem()] + [vmem()] * 4,
        out_specs=(vmem(), vmem()),
        compiler_params=params(),
        cost_estimate=pl.CostEstimate(flops=10**6, bytes_accessed=2 * 2**20, transcendentals=0),
        name="finish",
    )(place, own, from_a, from_b, terms)


def pair_swap(x, axis, odd_pairs):
    size = lax.axis_size(axis)
    first = 1 if odd_pairs else 0
    pairs = [(i, i + 1) for i in range(first, size - 1, 2)]
    return lax.ppermute(x, axis, pairs + [(j, i) for i, j in pairs])


def per_device(sky_cube, half_width, conv_weight, out_cotangent):
    freq_count, row_count, length = sky_cube.shape
    s, f = lax.axis_index("sky"), lax.axis_index("freq")
    place = jnp.stack([s, f]).astype(jnp.int32)
    s_even, f_even = s % 2 == 0, f % 2 == 0

    low_rows, high_rows = sky_cube[:, :HALF], sky_cube[:, HALF:]
    sky_b = pair_swap(jnp.where(s_even, low_rows, high_rows), "sky", True)
    sky_a = pair_swap(jnp.where(s_even, high_rows, low_rows), "sky", False)
    grad = back_project(conv_weight, out_cotangent)
    beam = beam_of(place, half_width, sky_cube, sky_a, sky_b)

    to_core = jnp.where(f_even, beam[3], beam[0])
    to_far = jnp.where(f_even, beam[0], beam[3])
    grad_core = jnp.where(f_even, grad[5], grad[0])
    grad_far = jnp.where(f_even, grad[0], grad[5])
    beam_far, add_far = pair_swap(to_far, "freq", True), pair_swap(grad_far, "freq", True)
    beam_core, add_core = pair_swap(to_core, "freq", False), pair_swap(grad_core, "freq", False)
    inner = inner_terms(beam, out_cotangent)

    own, up, down = spread(place, half_width, grad, add_core, add_far)
    row_b = pair_swap(jnp.where(s_even, up, down), "sky", True)
    row_a = pair_swap(jnp.where(s_even, down, up), "sky", False)
    copies = lax.axis_size("freq") * lax.axis_size("sky")
    terms = outer_terms(place, inner, beam_core, beam_far, out_cotangent, copies)
    gathered = lax.all_to_all(terms, ("freq", "sky"), 0, 0)
    cell_count = freq_count * lax.axis_size("freq") * row_count * lax.axis_size("sky") * length
    return finish(1.0 / math.sqrt(cell_count), place, own, row_a, row_b, gathered)


def solution(mesh):
    return jax.shard_map(
        per_device,
        mesh=mesh,
        in_specs=(P("freq", "sky", None), P("freq"), P(), P(None, "freq", "sky", None)),
        out_specs=(P("freq", "sky", None), P()),
        check_vma=False,
    )
```

profile of v0, /device:TPU:1, one launch (start us, length us, event | category | flops | bytes accessed | tf_op | source)
XLA Modules:
  0.0 64.1 jit_solution(13482930042693350183)
XLA Ops:
  0.6 1.0 %broadcast_select_fusion = (bf16[4,16,1024]{2,1,0:T(8,128)(2,1)S(1)}, bf16[4,16,1024]{2,1,0:T(8,128)(2,1)S(1)}) fusion(pred[]{:T(512)S(6)} %eq.10, bf16[4,32,1024]{2,1,0:T(8,128)(2,1)} %sky_ref.1), kind=kLoop, calls=%fused_computation.2 | loop fusion | flops 131072 | bytes 524289 | tf_op jit(solution)/shard_map/jit(_where)/select_n | solution.py:346
  1.6 2.5 %collective-permute-start.4 = (bf16[4,16,1024]{2,1,0:T(8,128)(2,1)S(1)}, bf16[4,16,1024]{2,1,0:T(8,128)(2,1)S(1)}, u32[]{:S(2)}, u32[]{:S(2)}) collective-permute-start(bf16[4,16,1024]{2,1,0:T(8,128)(2,1)S(1)} %get-tuple-element.15), channel_id=1, source_target_pairs={{0,1},{2,3},{4,5},{6,7},{8,9},{10,11},{12,13},{14,15},{16,17},{18,... | collective-permute-start | bytes 393224 | tf_op jit(solution)/shard_map/ppermute | solution.py:336
  4.2 0.7 %collective-permute-start.5 = (bf16[4,16,1024]{2,1,0:T(8,128)(2,1)S(1)}, bf16[4,16,1024]{2,1,0:T(8,128)(2,1)S(1)}, u32[]{:S(2)}, u32[]{:S(2)}) collective-permute-start(bf16[4,16,1024]{2,1,0:T(8,128)(2,1)S(1)} %get-tuple-element.14), channel_id=1, source_target_pairs={{1,2},{3,4},{5,6},{7,8},{9,10},{11,12},{13,14},{15,16},{17,18},{19... | collective-permute-start | bytes 393224 | tf_op jit(solution)/shard_map/ppermute | solution.py:336
  4.9 0.0 copy-start
  4.9 2.2 %copy-done = bf16[16,4,32,1024]{3,2,1,0:T(8,128)(2,1)S(1)} copy-done((bf16[16,4,32,1024]{3,2,1,0:T(8,128)(2,1)S(1)}, bf16[16,4,32,1024]{3,2,1,0:T(8,128)(2,1)}, u32[]{:S(2)}) %copy-start) | copy-done | bytes 4194328
  7.1 0.7 %copy-done.3 = bf16[16,27]{1,0:T(8,128)(2,1)S(1)} copy-done((bf16[16,27]{1,0:T(8,128)(2,1)S(1)}, bf16[16,27]{1,0:T(8,128)(2,1)}, u32[]{:S(2)}) %copy-start.3) | copy-done | bytes 888
  7.8 3.6 %back_project.1.grad_ref = f32[6,40,1024]{2,1,0:T(8,128)S(1)} custom-call(bf16[16,27]{1,0:T(8,128)(2,1)S(1)} %copy-done.3, bf16[16,4,32,1024]{3,2,1,0:T(8,128)(2,1)S(1)} %copy-done), custom_call_target="tpu_custom_call" | custom-call | flops 3000000000 | bytes 6291456 | tf_op jit(solution)/shard_map/back_project/pallas_call | solution.py:113
  11.4 0.0 copy-start.1
  11.4 1.0 %collective-permute-start = (f32[40,1024]{1,0:T(8,128)S(1)}, f32[40,1024]{1,0:T(8,128)S(1)}, u32[]{:S(2)}, u32[]{:S(2)}) collective-permute-start(f32[40,1024]{1,0:T(8,128)S(1)} %get-tuple-element.9), channel_id=1, source_target_pairs={{0,32},{64,96},{32,0},{96,64},{1,33},{65,97},{33,1},{97,65},{2,34}... | collective-permute-start | bytes 491528 | tf_op jit(solution)/shard_map/ppermute | solution.py:336
  12.4 4.8 %collective-permute-start.1 = (f32[40,1024]{1,0:T(8,128)S(1)}, f32[40,1024]{1,0:T(8,128)S(1)}, u32[]{:S(2)}, u32[]{:S(2)}) collective-permute-start(f32[40,1024]{1,0:T(8,128)S(1)} %get-tuple-element.8), channel_id=1, source_target_pairs={{32,64},{64,32},{33,65},{65,33},{34,66},{66,34},{35,67},{67,35},{3... | collective-permute-start | bytes 491528 | tf_op jit(solution)/shard_map/ppermute | solution.py:336
  17.3 0.1 pad_add_fusion.where_ref.refs_0_
  17.4 0.0 collective-permute-done.4.a_ref
  17.4 0.0 collective-permute-done.5.b_ref
  17.4 2.6 %beam.1.beam_ref = bf16[4,48,1024]{2,1,0:T(8,128)(2,1)S(1)} custom-call(s32[2]{0:T(128)S(1)} %pad_add_fusion.where_ref.refs_0_, s32[4]{0:T(128)S(1)} %copy-done.4, bf16[4,32,1024]{2,1,0:T(8,128)(2,1)S(1)} %copy-done.2, bf16[4,16,1024]{2,1,0:T(8,128)(2,1)S(1)} %collective-permute-done.4.a_ref, bf16[4,16,1024]{2,1,0:T(8,128)(2,1)S(1)} %collective-permute-done.5.b_ref), custom_call_target="tpu_custom_call" | custom-call | flops 2000000000 | bytes 1048576 | tf_op jit(solution)/shard_map/beam/pallas_call | solution.py:155
  20.0 0.1 collective-permute-start.6
  20.1 2.4 %collective-permute-start.7 = (bf16[48,1024]{1,0:T(8,128)(2,1)S(1)}, bf16[48,1024]{1,0:T(8,128)(2,1)S(1)}, u32[]{:S(2)}, u32[]{:S(2)}) collective-permute-start(bf16[48,1024]{1,0:T(8,128)(2,1)S(1)} %get-tuple-element.12), channel_id=1, source_target_pairs={{32,64},{64,32},{33,65},{65,33},{34,66},{66,34},{35,67},{67,35},{3... | collective-permute-start | bytes 294920 | tf_op jit(solution)/shard_map/ppermute | solution.py:336
  22.5 5.0 %inner_terms.1.inner_ref = f32[16,128]{1,0:T(8,128)S(1)} custom-call(bf16[4,48,1024]{2,1,0:T(8,128)(2,1)S(1)} %beam.1.beam_ref, bf16[16,4,32,1024]{3,2,1,0:T(8,128)(2,1)S(1)} %copy-done.1), custom_call_target="tpu_custom_call" | custom-call | flops 3000000000 | bytes 6291456 | tf_op jit(solution)/shard_map/inner_terms/pallas_call | solution.py:210
  27.5 3.0 %spread.1 = (f32[4,32,1024]{2,1,0:T(8,128)S(1)}, f32[4,16,1024]{2,1,0:T(8,128)S(1)}, f32[4,16,1024]{2,1,0:T(8,128)S(1)}) custom-call(s32[2]{0:T(128)S(1)} %pad_add_fusion.where_ref.refs_0_, s32[4]{0:T(128)S(1)} %copy-done.4, f32[6,40,1024]{2,1,0:T(8,128)S(1)} %back_project.1.grad_ref, f32[40,1024]{1,0:T(8,128)S(1)} %collective-permute-done.core_ref, ...), custom_call_target="tpu_custom_call" | custom-call | flops 3000000000 | bytes 3145728 | tf_op jit(solution)/shard_map/spread/pallas_call | solution.py:288
  30.6 4.5 %collective-permute-start.2 = (f32[4,16,1024]{2,1,0:T(8,128)S(1)}, f32[4,16,1024]{2,1,0:T(8,128)S(1)}, u32[]{:S(2)}, u32[]{:S(2)}) collective-permute-start(f32[4,16,1024]{2,1,0:T(8,128)S(1)} %get-tuple-element.11), channel_id=1, source_target_pairs={{0,1},{2,3},{4,5},{6,7},{8,9},{10,11},{12,13},{14,15},{16,17},{18,... | collective-permute-start | bytes 786440 | tf_op jit(solution)/shard_map/ppermute | solution.py:336
  35.0 0.7 %collective-permute-start.3 = (f32[4,16,1024]{2,1,0:T(8,128)S(1)}, f32[4,16,1024]{2,1,0:T(8,128)S(1)}, u32[]{:S(2)}, u32[]{:S(2)}) collective-permute-start(f32[4,16,1024]{2,1,0:T(8,128)S(1)} %get-tuple-element.10), channel_id=1, source_target_pairs={{1,2},{3,4},{5,6},{7,8},{9,10},{11,12},{13,14},{15,16},{17,18},{19... | collective-permute-start | bytes 786440 | tf_op jit(solution)/shard_map/ppermute | solution.py:336
  35.7 3.3 %outer_terms.1 = f32[128,4,128]{2,1,0:T(4,128)} custom-call(s32[2]{0:T(128)S(1)} %pad_add_fusion.where_ref.refs_0_, f32[16,128]{1,0:T(8,128)S(1)} %inner_terms.1.inner_ref, bf16[48,1024]{1,0:T(8,128)(2,1)S(1)} %collective-permute-done.6.core_ref, bf16[48,1024]{1,0:T(8,128)(2,1)S(1)} %collective-permute-done.7.far_ref, ...), custom_call_target="tpu_custom_call" | custom-call | flops 500000000 | bytes 3145728 | tf_op jit(solution)/shard_map/outer_terms/pallas_call | solution.py:242
  39.0 12.8 %all-to-all-start = ((f32[128,4,128]{2,1,0:T(4,128)}), f32[128,4,128]{2,1,0:T(4,128)S(1)}, u32[]{:S(2)}, u32[]{:S(2)}) async-start(f32[128,4,128]{2,1,0:T(4,128)} %outer_terms.1), calls=%async_computation | async-start | bytes 524288 | tf_op jit(solution)/shard_map/all_to_all | solution.py:364
  51.8 10.7 %all-to-all-done.refs_4_ = f32[128,4,128]{2,1,0:T(4,128)S(1)} async-done(((f32[128,4,128]{2,1,0:T(4,128)}), f32[128,4,128]{2,1,0:T(4,128)S(1)}, u32[]{:S(2)}, u32[]{:S(2)}) %all-to-all-start) | async-done | bytes 262176 | tf_op jit(solution)/shard_map/all_to_all | solution.py:364
  62.5 1.6 %finish.1 = (f32[4,32,1024]{2,1,0:T(8,128)}, f32[16,27]{1,0:T(8,128)}) custom-call(s32[2]{0:T(128)S(1)} %pad_add_fusion.where_ref.refs_0_, f32[4,32,1024]{2,1,0:T(8,128)S(1)} %get-tuple-element.5.refs_1_, f32[4,16,1024]{2,1,0:T(8,128)S(1)} %collective-permute-done.2.refs_2_, f32[4,16,1024]{2,1,0:T(8,128)S(1)} %collective-permute-done.3.refs_3_, ...), custom_call_target="tpu_custom_call" | custom-call | flops 1000000 | bytes 2097152 | tf_op jit(solution)/shard_map/finish/pallas_call | solution.py:321
  (15 shorter events, 0.1 us)
Async XLA Ops:
  1.6 15.7 %collective-permute-start.4 = (bf16[4,16,1024]{2,1,0:T(8,128)(2,1)S(1)}, bf16[4,16,1024]{2,1,0:T(8,128)(2,1)S(1)}, u32[]{:S(2)}, u32[]{:S(2)}) collective-permute-start(bf16[4,16,1024]{2,1,0:T(8,128)(2,1)S(1)} %get-tuple-element.15), channel_id=1, source_target_pairs={{0,1},{2,3},{4,5},{6,7},{8,9},{10,11},{12,13},{14,15},{16,17},{18,... | collective-permute-start | bytes 393224 | tf_op jit(solution)/shard_map/ppermute | solution.py:336
  4.2 13.2 %collective-permute-start.5 = (bf16[4,16,1024]{2,1,0:T(8,128)(2,1)S(1)}, bf16[4,16,1024]{2,1,0:T(8,128)(2,1)S(1)}, u32[]{:S(2)}, u32[]{:S(2)}) collective-permute-start(bf16[4,16,1024]{2,1,0:T(8,128)(2,1)S(1)} %get-tuple-element.14), channel_id=1, source_target_pairs={{1,2},{3,4},{5,6},{7,8},{9,10},{11,12},{13,14},{15,16},{17,18},{19... | collective-permute-start | bytes 393224 | tf_op jit(solution)/shard_map/ppermute | solution.py:336
  4.9 2.2 %copy-start = (bf16[16,4,32,1024]{3,2,1,0:T(8,128)(2,1)S(1)}, bf16[16,4,32,1024]{3,2,1,0:T(8,128)(2,1)}, u32[]{:S(2)}) copy-start(bf16[16,4,32,1024]{3,2,1,0:T(8,128)(2,1)} %last_ref.1) | copy-start | bytes 12582916
  7.1 0.7 %copy-start.3 = (bf16[16,27]{1,0:T(8,128)(2,1)S(1)}, bf16[16,27]{1,0:T(8,128)(2,1)}, u32[]{:S(2)}) copy-start(bf16[16,27]{1,0:T(8,128)(2,1)} %weight_ref.1) | copy-start | bytes 2596
  7.7 9.6 %copy-start.2 = (bf16[4,32,1024]{2,1,0:T(8,128)(2,1)S(1)}, bf16[4,32,1024]{2,1,0:T(8,128)(2,1)}, u32[]{:S(2)}) copy-start(bf16[4,32,1024]{2,1,0:T(8,128)(2,1)} %sky_ref.1) | copy-start | bytes 786436
  7.7 9.6 %copy-start.4 = (s32[4]{0:T(128)S(1)}, s32[4]{0:T(128)}, u32[]{:S(2)}) copy-start(s32[4]{0:T(128)} %width_ref.3) | copy-start | bytes 52
  11.4 11.1 %copy-start.1 = (bf16[16,4,32,1024]{3,2,1,0:T(8,128)(2,1)S(1)}, bf16[16,4,32,1024]{3,2,1,0:T(8,128)(2,1)}, u32[]{:S(2)}) copy-start(bf16[16,4,32,1024]{3,2,1,0:T(8,128)(2,1)} %last_ref.1) | copy-start | bytes 12582916
  11.4 16.1 %collective-permute-start = (f32[40,1024]{1,0:T(8,128)S(1)}, f32[40,1024]{1,0:T(8,128)S(1)}, u32[]{:S(2)}, u32[]{:S(2)}) collective-permute-start(f32[40,1024]{1,0:T(8,128)S(1)} %get-tuple-element.9), channel_id=1, source_target_pairs={{0,32},{64,96},{32,0},{96,64},{1,33},{65,97},{33,1},{97,65},{2,34}... | collective-permute-start | bytes 491528 | tf_op jit(solution)/shard_map/ppermute | solution.py:336
  12.4 15.1 %collective-permute-start.1 = (f32[40,1024]{1,0:T(8,128)S(1)}, f32[40,1024]{1,0:T(8,128)S(1)}, u32[]{:S(2)}, u32[]{:S(2)}) collective-permute-start(f32[40,1024]{1,0:T(8,128)S(1)} %get-tuple-element.8), channel_id=1, source_target_pairs={{32,64},{64,32},{33,65},{65,33},{34,66},{66,34},{35,67},{67,35},{3... | collective-permute-start | bytes 491528 | tf_op jit(solution)/shard_map/ppermute | solution.py:336
  20.0 15.7 %collective-permute-start.6 = (bf16[48,1024]{1,0:T(8,128)(2,1)S(1)}, bf16[48,1024]{1,0:T(8,128)(2,1)S(1)}, u32[]{:S(2)}, u32[]{:S(2)}) collective-permute-start(bf16[48,1024]{1,0:T(8,128)(2,1)S(1)} %get-tuple-element.13), channel_id=1, source_target_pairs={{0,32},{64,96},{32,0},{96,64},{1,33},{65,97},{33,1},{97,65},{2,34}... | collective-permute-start | bytes 294920 | tf_op jit(solution)/shard_map/ppermute | solution.py:336
  20.1 15.6 %collective-permute-start.7 = (bf16[48,1024]{1,0:T(8,128)(2,1)S(1)}, bf16[48,1024]{1,0:T(8,128)(2,1)S(1)}, u32[]{:S(2)}, u32[]{:S(2)}) collective-permute-start(bf16[48,1024]{1,0:T(8,128)(2,1)S(1)} %get-tuple-element.12), channel_id=1, source_target_pairs={{32,64},{64,32},{33,65},{65,33},{34,66},{66,34},{35,67},{67,35},{3... | collective-permute-start | bytes 294920 | tf_op jit(solution)/shard_map/ppermute | solution.py:336
  30.6 21.2 %collective-permute-start.2 = (f32[4,16,1024]{2,1,0:T(8,128)S(1)}, f32[4,16,1024]{2,1,0:T(8,128)S(1)}, u32[]{:S(2)}, u32[]{:S(2)}) collective-permute-start(f32[4,16,1024]{2,1,0:T(8,128)S(1)} %get-tuple-element.11), channel_id=1, source_target_pairs={{0,1},{2,3},{4,5},{6,7},{8,9},{10,11},{12,13},{14,15},{16,17},{18,... | collective-permute-start | bytes 786440 | tf_op jit(solution)/shard_map/ppermute | solution.py:336
  35.0 16.8 %collective-permute-start.3 = (f32[4,16,1024]{2,1,0:T(8,128)S(1)}, f32[4,16,1024]{2,1,0:T(8,128)S(1)}, u32[]{:S(2)}, u32[]{:S(2)}) collective-permute-start(f32[4,16,1024]{2,1,0:T(8,128)S(1)} %get-tuple-element.10), channel_id=1, source_target_pairs={{1,2},{3,4},{5,6},{7,8},{9,10},{11,12},{13,14},{15,16},{17,18},{19... | collective-permute-start | bytes 786440 | tf_op jit(solution)/shard_map/ppermute | solution.py:336
  39.0 23.6 %all-to-all-start = ((f32[128,4,128]{2,1,0:T(4,128)}), f32[128,4,128]{2,1,0:T(4,128)S(1)}, u32[]{:S(2)}, u32[]{:S(2)}) async-start(f32[128,4,128]{2,1,0:T(4,128)} %outer_terms.1), calls=%async_computation | async-start | bytes 524288 | tf_op jit(solution)/shard_map/all_to_all | solution.py:364
where the time goes:
time: 64.4 us; the launch traced here: 64.1 us
  starting transfers between devices  29.5 us (46%)
  Pallas kernels  19 us (30%)
  waiting for transfers between devices  10.7 us (17%)
  local copies, waits for them, and re-layouts  2.88 us (4%)
  other arithmetic  1.16 us (2%)
  between operations  0.85 us (1%)
    ppermute x8, starting transfers between devices, pair_swap(): return lax.ppermute(x, axis, pairs + [(j, i) for i, j in pairs])  16.6 us
    all_to_all x1, starting transfers between devices, per_device(): gathered = lax.all_to_all(terms, ('freq', 'sky'), 0, 0)  12.8 us
    all_to_all x1, waiting for transfers between devices, per_device(): gathered = lax.all_to_all(terms, ('freq', 'sky'), 0, 0)  10.7 us
    pallas_call x1, Pallas kernels, inner_terms(): pl.pallas_call(inner_kernel, grid=(4,), out_shape=jax.ShapeDtypeStruct((1...  4.98 us
    pallas_call x1, Pallas kernels, back_project(): pl.pallas_call(back_kernel, grid=(4,), out_shape=jax.ShapeDtypeStruct((6,...  3.61 us
    pallas_call x1, Pallas kernels, outer_terms(): pl.pallas_call(outer_kernel, grid=(1,), out_shape=jax.ShapeDtypeStruct((c...  3.25 us
    pallas_call x1, Pallas kernels, spread(): pl.pallas_call(spread_kernel, out_shape=(jax.ShapeDtypeStruct((4, 32, 102...  3 us
    unnamed x10, local copies, waits for them, and re-layouts  2.88 us
  transfers between devices with their start and end apart: 9, of which 1 were waited for; matrix products, arithmetic and copies ran while one was open for 0% of the time, Pallas kernels for 27%

commit v1 on v0

v1 whole, which is shorter than its diff:
```python
import math

import jax
import jax.numpy as jnp
from jax import lax
from jax.experimental import pallas as pl
from jax.experimental.pallas import tpu as pltpu
from jax.sharding import PartitionSpec as P

MAXH = 12
HALF = 16
F32 = jnp.float32
BF16 = jnp.bfloat16
MIB = 1024 * 1024


def params(mib=24):
    return pltpu.CompilerParams(vmem_limit_bytes=mib * MIB)


def iota(shape, dim):
    return lax.broadcasted_iota(jnp.int32, shape, dim)


def dot(a, b):
    return jnp.dot(a, b, preferred_element_type=F32)


def split(x):
    hi = x.astype(BF16)
    return hi, (x - hi.astype(F32)).astype(BF16)


def taps_at(offsets, width):
    def profile(d):
        w = jnp.full(d.shape, width, jnp.int32)
        wf = w.astype(F32)
        df = d.astype(F32)
        return jnp.where(jnp.abs(d) <= w, jnp.exp(-2.0 * (df * df) / (wf * wf)), 0.0)

    line = profile(iota((8, 128), 1) - 64)
    norm = jnp.sqrt(jnp.sum(line * line, axis=1, keepdims=True))[:1]
    return profile(offsets) / norm


def column_matrices(width):
    band = taps_at(iota((160, 128), 0) - 16 - iota((160, 128), 1), width)
    left = jnp.concatenate([jnp.zeros((112, 128), F32), band, jnp.zeros((240, 128), F32)], axis=0)
    right = jnp.concatenate([jnp.zeros((240, 128), F32), band, jnp.zeros((112, 128), F32)], axis=0)
    return split(jnp.concatenate([left, right], axis=1))


def blur_columns(rows, hi, lo):
    n = rows.shape[0]
    edge = jnp.zeros((n, 128), BF16)
    padded = jnp.concatenate([edge, rows, edge], axis=1)
    stacked = jnp.concatenate([padded[:, 256 * j : 256 * j + 512] for j in range(4)], axis=0)
    out = dot(stacked, hi) + dot(stacked, lo)
    return jnp.concatenate([out[n * j : n * j + n] for j in range(4)], axis=1)


def row_matrix(count, n, base, width):
    hi, lo = split(taps_at(iota((count, n), 1) - iota((count, n), 0) - base, width))
    hi, lo = hi.astype(F32), lo.astype(F32)
    return jnp.concatenate([hi, hi, lo], axis=1).astype(BF16)


def three_parts(source):
    hi = source.astype(BF16).astype(F32)
    return jnp.concatenate([hi, source - hi, hi], axis=0).astype(BF16)


def shift_cols(x, offset):
    if offset == 0:
        return x
    length = x.shape[-1]
    col = iota(x.shape, x.ndim - 1)
    if offset > 0:
        return jnp.where(col < length - 1, pltpu.roll(x, length - 1, x.ndim - 1), 0.0)
    return jnp.where(col > 0, pltpu.roll(x, 1, x.ndim - 1), 0.0)


def vmem():
    return pl.BlockSpec(memory_space=pltpu.VMEM)


def hbm():
    return pl.BlockSpec(memory_space=pltpu.HBM)


def plane_copies(cot_ref, planes, held, sem):
    return [pltpu.make_async_copy(cot_ref.at[:, f], held.at[i], sem.at[i]) for i, f in enumerate(planes)]


def back_kernel(
    width_hbm, weight_hbm, cot_ref, out_ref, mats_ref, held, acc_ref, weight_ref, width_ref, sem
):
    small = [
        pltpu.make_async_copy(weight_hbm, weight_ref, sem.at[4]),
        pltpu.make_async_copy(width_hbm, width_ref, sem.at[5]),
    ]
    for copy in small:
        copy.start()
    copies = plane_copies(cot_ref, range(4), held, sem)
    for copy in copies:
        copy.start()
    small[0].wait()
    small[1].wait()
    expand = (iota((16, 512), 1) // 32 == iota((16, 512), 0)).astype(BF16)
    w = lax.dot_general(weight_ref[...], expand, (((0,), (0,)), ((), ())), preferred_element_type=F32)
    diff = iota((40, 512), 0) - iota((40, 512), 1) % 32
    blocks = []
    for a in range(3):
        for e in range(3):
            block = jnp.zeros((40, 512), F32)
            for b in range(3):
                row = w[9 * a + 3 * b + e : 9 * a + 3 * b + e + 1, :]
                block = jnp.where(diff == b, row, block)
            blocks.append(block)
    matrix = jnp.concatenate(blocks, axis=0).astype(BF16)
    for f in range(4):
        width = width_ref[f]
        mats_ref[f, :512], mats_ref[f, 512:1024] = column_matrices(width)
        mats_ref[f, 1024:1072, :192] = row_matrix(48, 64, 15, width)
        mats_ref[f, 1072:, :120] = row_matrix(64, 40, -15, width)
    for f in range(4):
        copies[f].wait()
        terms = dot(matrix, held[f].reshape(512, 1024))
        for a in range(3):
            part = terms[120 * a : 120 * a + 120]
            if f == 0 or a == 2:
                acc_ref[f + a] = part
            else:
                acc_ref[f + a] += part
    for p in range(6):
        full = acc_ref[p]
        out_ref[p] = shift_cols(full[0:40], 1) + full[40:80] + shift_cols(full[80:120], -1)


def back_project(half_width, conv_weight, out_cotangent):
    return pl.pallas_call(
        back_kernel,
        out_shape=(
            jax.ShapeDtypeStruct((6, 40, 1024), F32),
            jax.ShapeDtypeStruct((4, 1136, 256), BF16),
            jax.ShapeDtypeStruct((4, 16, 32, 1024), BF16),
        ),
        in_specs=[hbm(), hbm(), hbm()],
        out_specs=(vmem(),) * 3,
        scratch_shapes=[
            pltpu.VMEM((6, 120, 1024), F32),
            pltpu.VMEM((16, 27), BF16),
            pltpu.SMEM((4,), jnp.int32),
            pltpu.SemaphoreType.DMA((6,)),
        ],
        compiler_params=params(),
        cost_estimate=pl.CostEstimate(flops=3 * 10**9, bytes_accessed=7 * 2**20, transcendentals=10**5),
        name="back_project",
    )(half_width, conv_weight, out_cotangent)


def beam_kernel(mats_ref, sky_ref, a_ref, b_ref, grad_ref, beam_ref, core_ref, far_ref):
    even = lax.axis_index("sky") % 2 == 0
    f_even = lax.axis_index("freq") % 2 == 0
    row = iota((48, 1024), 0)
    first = jnp.where(lax.axis_index("sky") == 0, 1, 0)
    last = jnp.where(lax.axis_index("sky") == lax.axis_size("sky") - 1, 33, 34)
    keep = (row >= first) & (row < last)
    smooth = []
    for f in range(4):
        ra, rb = a_ref[f], b_ref[f]
        above = jnp.where(even, rb, ra)
        below = jnp.where(even, ra, rb)
        rows = jnp.concatenate([above, sky_ref[f], below], axis=0)
        smooth.append(three_parts(blur_columns(rows, mats_ref[f, :512], mats_ref[f, 512:1024])))
    beams = [jnp.where(keep, dot(mats_ref[f, 1024:1072, :192], smooth[f]), 0.0) for f in range(4)]
    for f in range(4):
        beam_ref[f] = beams[f].astype(BF16)
    edges = []
    for f, p in ((0, 0), (3, 5)):
        g = grad_ref[p]
        high = g.astype(BF16).astype(F32)
        edges.append(jnp.concatenate([beams[f], high, g - high], axis=0))
    core_ref[...] = jnp.where(f_even, edges[1], edges[0]).astype(BF16)
    far_ref[...] = jnp.where(f_even, edges[0], edges[1]).astype(BF16)


def beam_of(mats, sky_cube, from_a, from_b, grad):
    edge = jax.ShapeDtypeStruct((128, 1024), BF16)
    return pl.pallas_call(
        beam_kernel,
        out_shape=(jax.ShapeDtypeStruct((4, 48, 1024), BF16), edge, edge),
        in_specs=[vmem()] * 5,
        out_specs=(vmem(), vmem(), vmem()),
        compiler_params=params(),
        cost_estimate=pl.CostEstimate(flops=10**9, bytes_accessed=4 * 2**20, transcendentals=0),
        name="beam",
    )(mats, sky_cube, from_a, from_b, grad)


def three_shifts(beam):
    wide = beam[:40].astype(F32)
    parts = [shift_cols(wide, e - 1) for e in range(3)] + [jnp.zeros((8, beam.shape[1]), F32)]
    return jnp.concatenate(parts, axis=0).astype(BF16)


def contract(a, b):
    return lax.dot_general(a, b, (((1,), (1,)), ((), ())), preferred_element_type=F32)


def inner_kernel(beam_ref, cot_ref, out_ref, shift_ref):
    for p in range(4):
        shift_ref[pl.ds(128 * p, 128)] = three_shifts(beam_ref[p])
    for f in (1, 0, 2, 3):
        low, high = max(f - 1, 0), min(f + 2, 4)
        terms = contract(cot_ref[f].reshape(512, 1024), shift_ref[pl.ds(128 * low, 128 * (high - low))])
        cols = pl.ds(128 * (low - f + 1), 128 * (high - low))
        if f == 1:
            out_ref[:, cols] = terms
        else:
            out_ref[:, cols] += terms


def inner_terms(beam, out_cotangent):
    return pl.pallas_call(
        inner_kernel,
        out_shape=jax.ShapeDtypeStruct((512, 384), F32),
        in_specs=[vmem(), vmem()],
        out_specs=vmem(),
        scratch_shapes=[pltpu.VMEM((512, 1024), BF16)],
        compiler_params=params(),
        cost_estimate=pl.CostEstimate(flops=2 * 10**9, bytes_accessed=6 * 2**20, transcendentals=0),
        name="inner_terms",
    )(beam, out_cotangent)


def outer_kernel(gram_ref, core_ref, far_ref, cot_ref, out_ref):
    even = lax.axis_index("freq") % 2 == 0
    core, far = core_ref[:48], far_ref[:48]
    before = three_shifts(jnp.where(even, far, core))
    after = three_shifts(jnp.where(even, core, far))
    low = contract(cot_ref[0].reshape(512, 1024), before) + gram_ref[:, :128]
    high = contract(cot_ref[3].reshape(512, 1024), after) + gram_ref[:, 256:]
    gram = jnp.concatenate([low, gram_ref[:, 128:256], high], axis=1).reshape(16, 32, 384)
    col = iota((32, 384), 1) % 128
    e = col // 40
    diff = col - 40 * e - iota((32, 384), 0)
    parts = [jnp.where((diff == b)[None], gram, 0.0).sum(axis=1) for b in range(3)]
    sums = jnp.concatenate(parts, axis=1)
    top, rest = split(sums)
    rest = sums - top.astype(F32)
    mid = rest.astype(BF16)
    low_part = (rest - mid.astype(F32)).astype(BF16)
    n = iota((1152, 128), 0)
    b, a, e = n // 384, n % 384 // 128, n % 128 // 40
    chosen = (iota((1152, 128), 1) % 32 == jnp.where(e < 3, 9 * a + 3 * b + e, 99)).astype(F32).astype(BF16)
    total = dot(top, chosen) + (dot(mid, chosen) + dot(low_part, chosen))
    placed = jnp.where(iota((16, 128), 1) // 32 == iota((16, 128), 0) % 4, total, 0.0)
    packed = placed.reshape(4, 4, 128).sum(axis=1)
    out_ref[...] = jnp.broadcast_to(packed[None], out_ref.shape)


def outer_terms(gram, from_core, from_far, out_cotangent, copies):
    return pl.pallas_call(
        outer_kernel,
        out_shape=jax.ShapeDtypeStruct((copies, 4, 128), F32),
        in_specs=[vmem()] * 4,
        out_specs=vmem(),
        compiler_params=params(),
        cost_estimate=pl.CostEstimate(flops=5 * 10**8, bytes_accessed=3 * 2**20, transcendentals=0),
        name="outer_terms",
    )(gram, from_core, from_far, out_cotangent)


def spread_kernel(mats_ref, grad_ref, core_ref, far_ref, own_ref, to_a_ref, to_b_ref):
    s_even = lax.axis_index("sky") % 2 == 0
    even = lax.axis_index("freq") % 2 == 0
    core = core_ref[48:88].astype(F32) + core_ref[88:].astype(F32)
    far = far_ref[48:88].astype(F32) + far_ref[88:].astype(F32)
    row = iota((40, 1024), 0)
    first = jnp.where(lax.axis_index("sky") == 0, 1, 0)
    last = jnp.where(lax.axis_index("sky") == lax.axis_size("sky") - 1, 33, 34)
    keep = (row >= first) & (row < last)
    shared = (row < 2) | (row >= 32)
    smooth = []
    for f in range(4):
        grad = grad_ref[f + 1]
        if f == 0:
            grad = grad + jnp.where(even, far, core)
        if f == 3:
            grad = grad + jnp.where(even, core, far)
        grad = jnp.where(keep, grad, 0.0)
        hi = grad.astype(BF16).astype(F32)
        lo = jnp.where(shared, grad - hi, 0.0)
        both = blur_columns(jnp.concatenate([hi, lo], axis=0).astype(BF16), mats_ref[f, :512], mats_ref[f, 512:1024])
        smooth.append(three_parts(both[:40] + both[40:]))
    for f in range(4):
        out = dot(mats_ref[f, 1072:, :120], smooth[f])
        own_ref[f] = out[16:48]
        to_a_ref[f] = jnp.where(s_even, out[48:], out[:16])
        to_b_ref[f] = jnp.where(s_even, out[:16], out[48:])


def spread(mats, grad, from_core, from_far):
    edge = jax.ShapeDtypeStruct((4, HALF, 1024), F32)
    return pl.pallas_call(
        spread_kernel,
        out_shape=(jax.ShapeDtypeStruct((4, 32, 1024), F32), edge, edge),
        in_specs=[vmem()] * 4,
        out_specs=(vmem(), vmem(), vmem()),
        compiler_params=params(),
        cost_estimate=pl.CostEstimate(flops=10**9, bytes_accessed=3 * 2**20, transcendentals=0),
        name="spread",
    )(mats, grad, from_core, from_far)


def final_kernel(scale, own_ref, a_ref, b_ref, terms_ref, sky_ref, grad_ref):
    even = lax.axis_index("sky") % 2 == 0
    for f in range(4):
        ra, rb = a_ref[f], b_ref[f]
        sky_ref[f, :HALF] = own_ref[f, :HALF] + jnp.where(even, rb, ra)
        sky_ref[f, HALF:] = own_ref[f, HALF:] + jnp.where(even, ra, rb)
    packed = jnp.sum(terms_ref[...], axis=0) * scale
    rows = jnp.broadcast_to(packed[:, None, :], (4, 4, 128)).reshape(16, 128)
    placed = jnp.where(iota((16, 128), 1) // 32 == iota((16, 128), 0) % 4, rows, 0.0)
    fold = (iota((128, 128), 0) % 32 == iota((128, 128), 1)).astype(F32)
    out = jnp.dot(placed, fold, preferred_element_type=F32, precision=lax.Precision.HIGHEST)
    grad_ref[...] = out[:, :27]


def finish(scale, own, from_a, from_b, terms):
    def body(*refs):
        final_kernel(scale, *refs)

    return pl.pallas_call(
        body,
        out_shape=(jax.ShapeDtypeStruct((4, 32, 1024), F32), jax.ShapeDtypeStruct((16, 27), F32)),
        in_specs=[vmem()] * 4,
        out_specs=(vmem(), vmem()),
        compiler_params=params(),
        cost_estimate=pl.CostEstimate(flops=10**6, bytes_accessed=2 * 2**20, transcendentals=0),
        name="finish",
    )(own, from_a, from_b, terms)


def pair_swap(x, axis, odd_pairs):
    size = lax.axis_size(axis)
    first = 1 if odd_pairs else 0
    pairs = [(i, i + 1) for i in range(first, size - 1, 2)]
    return lax.ppermute(x, axis, pairs + [(j, i) for i, j in pairs])


def per_device(sky_cube, half_width, conv_weight, out_cotangent):
    freq_count, row_count, length = sky_cube.shape
    s_even = lax.axis_index("sky") % 2 == 0
    out_cotangent, conv_weight, half_width = (
        pltpu.with_memory_space_constraint(x, pltpu.HBM) for x in (out_cotangent, conv_weight, half_width)
    )

    low_rows, high_rows = sky_cube[:, :HALF], sky_cube[:, HALF:]
    sky_a = pair_swap(jnp.where(s_even, high_rows, low_rows), "sky", False)
    sky_b = pair_swap(jnp.where(s_even, low_rows, high_rows), "sky", True)
    grad, mats, held = back_project(half_width, conv_weight, out_cotangent)
    beam, to_core, to_far = beam_of(mats, sky_cube, sky_a, sky_b, grad)
    from_core, from_far = pair_swap(to_core, "freq", False), pair_swap(to_far, "freq", True)
    gram = inner_terms(beam, held)
    own, to_a, to_b = spread(mats, grad, from_core, from_far)
    row_a, row_b = pair_swap(to_a, "sky", False), pair_swap(to_b, "sky", True)
    copies = lax.axis_size("freq") * lax.axis_size("sky")
    terms = outer_terms(gram, from_core, from_far, held, copies)
    gathered = lax.all_to_all(terms, ("freq", "sky"), 0, 0)
    cell_count = freq_count * lax.axis_size("freq") * row_count * lax.axis_size("sky") * length
    return finish(1.0 / math.sqrt(cell_count), own, row_a, row_b, gathered)


def solution(mesh):
    return jax.shard_map(
        per_device,
        mesh=mesh,
        in_specs=(P("freq", "sky", None), P("freq"), P(), P(None, "freq", "sky", None)),
        out_specs=(P("freq", "sky", None), P()),
        check_vma=False,
    )
```

time: 64.4 us -> 53.6 us (0.83)
  blocking collectives: 0 us -> 24 us
  starting transfers between devices: 29.5 us -> 14.2 us
  Pallas kernels: 19 us -> 10.8 us
  waiting for transfers between devices: 10.7 us -> 2.73 us
  local copies, waits for them, and re-layouts: 2.88 us -> 0.01 us
    all_to_all x0 -> x1, blocking collectives: none -> 24 us  [per_device(): gathered = lax.all_to_all(terms, ('freq', 'sky'), 0, 0)]
    all_to_all x1 -> x0, starting transfers between devices: 12.8 us -> none  [per_device(): gathered = lax.all_to_all(terms, ('freq', 'sky'), 0, 0)]
    all_to_all x1 -> x0, waiting for transfers between devices: 10.7 us -> none  [per_device(): gathered = lax.all_to_all(terms, ('freq', 'sky'), 0, 0)]
    pallas_call x4, Pallas kernels: 14.5 us -> 8.68 us  [the longest x1 3.75 us: back_project(): pl.pallas_call(back_kernel, out_shape=(jax.ShapeDtypeStruct((6, 40, 1024)...]
    unnamed x10 -> x2, local copies, waits for them, and re-layouts: 2.88 us -> 0.01 us
    ppermute x8 -> x6, waiting for transfers between devices: 0.02 us -> 2.73 us  [pair_swap(): return lax.ppermute(x, axis, pairs + [(j, i) for i, j in pairs])]
    ppermute x8 -> x6, starting transfers between devices: 16.6 us -> 14.2 us  [pair_swap(): return lax.ppermute(x, axis, pairs + [(j, i) for i, j in pairs])]
    pallas_call x1, Pallas kernels: 3 us -> 1.03 us  [spread(): pl.pallas_call(spread_kernel, out_shape=(jax.ShapeDtypeStruct((4, 32, 102...]
  transfers between devices with their start and end apart: 9 -> 6, of which waited for: 1 -> 1; matrix products, arithmetic and copies ran while one was open for 0% -> 0% of each run, Pallas kernels for 27% -> 14%
where the time goes in v1:
time: 53.6 us; the launch traced here: 53.4 us
  blocking collectives  24 us (45%)
  starting transfers between devices  14.2 us (26%)
  Pallas kernels  10.8 us (20%)
  waiting for transfers between devices  2.73 us (5%)
  other arithmetic  1 us (2%)
  between operations  0.74 us (1%)
    all_to_all x1, blocking collectives, per_device(): gathered = lax.all_to_all(terms, ('freq', 'sky'), 0, 0)  24 us
    ppermute x6, starting transfers between devices, pair_swap(): return lax.ppermute(x, axis, pairs + [(j, i) for i, j in pairs])  14.2 us
    pallas_call x1, Pallas kernels, back_project(): pl.pallas_call(back_kernel, out_shape=(jax.ShapeDtypeStruct((6, 40, 1024)...  3.75 us
    ppermute x6, waiting for transfers between devices, pair_swap(): return lax.ppermute(x, axis, pairs + [(j, i) for i, j in pairs])  2.73 us
    pallas_call x1, Pallas kernels, outer_terms(): pl.pallas_call(outer_kernel, out_shape=jax.ShapeDtypeStruct((copies, 4, 1...  2.05 us
    pallas_call x1, Pallas kernels, inner_terms(): pl.pallas_call(inner_kernel, out_shape=jax.ShapeDtypeStruct((512, 384), F...  1.89 us
  transfers between devices with their start and end apart: 6, of which 1 were waited for; matrix products, arithmetic and copies ran while one was open for 0% of the time, Pallas kernels for 14%

profile of v1, /device:TPU:1, one launch (start us, length us, event | category | flops | bytes accessed | tf_op | source)
XLA Modules:
  0.0 53.4 jit_solution(14038070033861578131)
XLA Ops:
  0.6 1.0 %broadcast_select_fusion = (bf16[4,16,1024]{2,1,0:T(8,128)(2,1)S(1)}, bf16[4,16,1024]{2,1,0:T(8,128)(2,1)S(1)}) fusion(pred[]{:T(512)S(6)} %eq.5, bf16[4,32,1024]{2,1,0:T(8,128)(2,1)} %sky_ref.1), kind=kLoop, calls=%fused_computation | loop fusion | flops 131072 | bytes 524289 | tf_op jit(solution)/shard_map/jit(_where)/select_n | solution.py:362
  1.6 2.5 %collective-permute-start = (bf16[4,16,1024]{2,1,0:T(8,128)(2,1)S(1)}, bf16[4,16,1024]{2,1,0:T(8,128)(2,1)S(1)}, u32[]{:S(2)}, u32[]{:S(2)}) collective-permute-start(bf16[4,16,1024]{2,1,0:T(8,128)(2,1)S(1)} %get-tuple-element.21), channel_id=1, source_target_pairs={{0,1},{2,3},{4,5},{6,7},{8,9},{10,11},{12,13},{14,15},{16,17},{18,... | collective-permute-start | bytes 393224 | tf_op jit(solution)/shard_map/ppermute | solution.py:350
  4.2 0.0 copy-start
  4.2 0.8 %collective-permute-start.1 = (bf16[4,16,1024]{2,1,0:T(8,128)(2,1)S(1)}, bf16[4,16,1024]{2,1,0:T(8,128)(2,1)S(1)}, u32[]{:S(2)}, u32[]{:S(2)}) collective-permute-start(bf16[4,16,1024]{2,1,0:T(8,128)(2,1)S(1)} %get-tuple-element.20), channel_id=1, source_target_pairs={{1,2},{3,4},{5,6},{7,8},{9,10},{11,12},{13,14},{15,16},{17,18},{19... | collective-permute-start | bytes 393224 | tf_op jit(solution)/shard_map/ppermute | solution.py:350
  5.0 3.7 %back_project.1 = (f32[6,40,1024]{2,1,0:T(8,128)S(1)}, bf16[4,1136,256]{2,1,0:T(8,128)(2,1)S(1)}, bf16[4,16,32,1024]{3,2,1,0:T(8,128)(2,1)S(1)}) custom-call(s32[4]{0:T(128)} %width_hbm.1, bf16[16,27]{1,0:T(8,128)(2,1)} %weight_hbm.1, bf16[16,4,32,1024]{3,2,1,0:T(8,128)(2,1)} %cot_ref.1), custom_call_target="tpu_custom_call" | custom-call | flops 3000000000 | bytes 7340032 | tf_op jit(solution)/shard_map/back_project/pallas_call | solution.py:141
  8.7 0.0 collective-permute-done.a_ref
  8.8 0.0 collective-permute-done.1.b_ref
  8.8 0.0 copy-done
  8.8 1.0 %beam.1 = (bf16[4,48,1024]{2,1,0:T(8,128)(2,1)S(1)}, bf16[128,1024]{1,0:T(8,128)(2,1)S(1)}, bf16[128,1024]{1,0:T(8,128)(2,1)S(1)}) custom-call(bf16[4,1136,256]{2,1,0:T(8,128)(2,1)S(1)} %get-tuple-element.11.mats_ref, bf16[4,32,1024]{2,1,0:T(8,128)(2,1)S(1)} %copy-done, bf16[4,16,1024]{2,1,0:T(8,128)(2,1)S(1)} %collective-permute-done.a_ref, ...), custom_call_target="tpu_custom_call" | custom-call | flops 1000000000 | bytes 4194304 | tf_op jit(solution)/shard_map/beam/pallas_call | solution.py:190
  9.8 1.0 %collective-permute-start.2 = (bf16[128,1024]{1,0:T(8,128)(2,1)S(1)}, bf16[128,1024]{1,0:T(8,128)(2,1)S(1)}, u32[]{:S(2)}, u32[]{:S(2)}) collective-permute-start(bf16[128,1024]{1,0:T(8,128)(2,1)S(1)} %get-tuple-element.13), channel_id=1, source_target_pairs={{0,32},{64,96},{32,0},{96,64},{1,33},{65,97},{33,1},{97,65},{2,34}... | collective-permute-start | bytes 786440 | tf_op jit(solution)/shard_map/ppermute | solution.py:350
  10.8 4.5 %collective-permute-start.3 = (bf16[128,1024]{1,0:T(8,128)(2,1)S(1)}, bf16[128,1024]{1,0:T(8,128)(2,1)S(1)}, u32[]{:S(2)}, u32[]{:S(2)}) collective-permute-start(bf16[128,1024]{1,0:T(8,128)(2,1)S(1)} %get-tuple-element.14), channel_id=1, source_target_pairs={{32,64},{64,32},{33,65},{65,33},{34,66},{66,34},{35,67},{67,35},{3... | collective-permute-start | bytes 786440 | tf_op jit(solution)/shard_map/ppermute | solution.py:350
  15.4 1.9 %inner_terms.1.gram_ref = f32[512,384]{1,0:T(8,128)S(1)} custom-call(bf16[4,48,1024]{2,1,0:T(8,128)(2,1)S(1)} %get-tuple-element.18.beam_ref, bf16[4,16,32,1024]{3,2,1,0:T(8,128)(2,1)S(1)} %get-tuple-element.19.cot_ref), custom_call_target="tpu_custom_call" | custom-call | flops 2000000000 | bytes 6291456 | tf_op jit(solution)/shard_map/inner_terms/pallas_call | solution.py:225
  17.3 0.0 collective-permute-done.2.core_ref
  17.3 2.7 %collective-permute-done.3.far_ref = bf16[128,1024]{1,0:T(8,128)(2,1)S(1)} collective-permute-done((bf16[128,1024]{1,0:T(8,128)(2,1)S(1)}, bf16[128,1024]{1,0:T(8,128)(2,1)S(1)}, u32[]{:S(2)}, u32[]{:S(2)}) %collective-permute-start.3) | collective-permute-done | bytes 262176 | tf_op jit(solution)/shard_map/ppermute | solution.py:350
  20.0 1.0 %spread.1 = (f32[4,32,1024]{2,1,0:T(8,128)S(1)}, f32[4,16,1024]{2,1,0:T(8,128)S(1)}, f32[4,16,1024]{2,1,0:T(8,128)S(1)}) custom-call(bf16[4,1136,256]{2,1,0:T(8,128)(2,1)S(1)} %get-tuple-element.11.mats_ref, f32[6,40,1024]{2,1,0:T(8,128)S(1)} %get-tuple-element.12.grad_ref, bf16[128,1024]{1,0:T(8,128)(2,1)S(1)} %collective-permute-done.2.core_ref, ...), custom_call_target="tpu_custom_call" | custom-call | flops 1000000000 | bytes 3145728 | tf_op jit(solution)/shard_map/spread/pallas_call | solution.py:306
  21.0 4.6 %collective-permute-start.4 = (f32[4,16,1024]{2,1,0:T(8,128)S(1)}, f32[4,16,1024]{2,1,0:T(8,128)S(1)}, u32[]{:S(2)}, u32[]{:S(2)}) collective-permute-start(f32[4,16,1024]{2,1,0:T(8,128)S(1)} %get-tuple-element.16), channel_id=1, source_target_pairs={{0,1},{2,3},{4,5},{6,7},{8,9},{10,11},{12,13},{14,15},{16,17},{18,... | collective-permute-start | bytes 786440 | tf_op jit(solution)/shard_map/ppermute | solution.py:350
  25.6 0.7 %collective-permute-start.5 = (f32[4,16,1024]{2,1,0:T(8,128)S(1)}, f32[4,16,1024]{2,1,0:T(8,128)S(1)}, u32[]{:S(2)}, u32[]{:S(2)}) collective-permute-start(f32[4,16,1024]{2,1,0:T(8,128)S(1)} %get-tuple-element.17), channel_id=1, source_target_pairs={{1,2},{3,4},{5,6},{7,8},{9,10},{11,12},{13,14},{15,16},{17,18},{19... | collective-permute-start | bytes 786440 | tf_op jit(solution)/shard_map/ppermute | solution.py:350
  26.3 2.1 %outer_terms.1 = f32[128,4,128]{2,1,0:T(4,128)S(1)} custom-call(f32[512,384]{1,0:T(8,128)S(1)} %inner_terms.1.gram_ref, bf16[128,1024]{1,0:T(8,128)(2,1)S(1)} %collective-permute-done.2.core_ref, bf16[128,1024]{1,0:T(8,128)(2,1)S(1)} %collective-permute-done.3.far_ref, bf16[4,16,32,1024]{3,2,1,0:T(8,128)(2,1)S(1)} %get-tuple-element.19.cot_ref), custom_call_target="tpu_custom_call" | custom-call | flops 500000000 | bytes 3145728 | tf_op jit(solution)/shard_map/outer_terms/pallas_call | solution.py:264
  28.3 24.0 %all_to_all.5.refs_3_ = f32[128,4,128]{2,1,0:T(4,128)S(1)} all-to-all(f32[128,4,128]{2,1,0:T(4,128)S(1)} %outer_terms.1), channel_id=1, replica_groups=mesh['freq'=4,'sky'=32] {'freq','sky'}, dimensions={0} | all-to-all | bytes 524288 | tf_op jit(solution)/shard_map/all_to_all | solution.py:371
  52.3 0.0 collective-permute-done.4.refs_1_
  52.3 0.0 collective-permute-done.5.refs_2_
  52.3 1.0 %finish.1 = (f32[4,32,1024]{2,1,0:T(8,128)}, f32[16,27]{1,0:T(8,128)}) custom-call(f32[4,32,1024]{2,1,0:T(8,128)S(1)} %get-tuple-element.15.refs_0_, f32[4,16,1024]{2,1,0:T(8,128)S(1)} %collective-permute-done.4.refs_1_, f32[4,16,1024]{2,1,0:T(8,128)S(1)} %collective-permute-done.5.refs_2_, f32[128,4,128]{2,1,0:T(4,128)S(1)} %all_to_all.5.refs_3_), custom_call_target="tpu_custom_call" | custom-call | flops 1000000 | bytes 2097152 | tf_op jit(solution)/shard_map/finish/pallas_call | solution.py:335
Async XLA Ops:
  1.6 7.1 %collective-permute-start = (bf16[4,16,1024]{2,1,0:T(8,128)(2,1)S(1)}, bf16[4,16,1024]{2,1,0:T(8,128)(2,1)S(1)}, u32[]{:S(2)}, u32[]{:S(2)}) collective-permute-start(bf16[4,16,1024]{2,1,0:T(8,128)(2,1)S(1)} %get-tuple-element.21), channel_id=1, source_target_pairs={{0,1},{2,3},{4,5},{6,7},{8,9},{10,11},{12,13},{14,15},{16,17},{18,... | collective-permute-start | bytes 393224 | tf_op jit(solution)/shard_map/ppermute | solution.py:350
  4.2 4.6 %copy-start = (bf16[4,32,1024]{2,1,0:T(8,128)(2,1)S(1)}, bf16[4,32,1024]{2,1,0:T(8,128)(2,1)}, u32[]{:S(2)}) copy-start(bf16[4,32,1024]{2,1,0:T(8,128)(2,1)} %sky_ref.1) | copy-start | bytes 786436
  4.2 4.6 %collective-permute-start.1 = (bf16[4,16,1024]{2,1,0:T(8,128)(2,1)S(1)}, bf16[4,16,1024]{2,1,0:T(8,128)(2,1)S(1)}, u32[]{:S(2)}, u32[]{:S(2)}) collective-permute-start(bf16[4,16,1024]{2,1,0:T(8,128)(2,1)S(1)} %get-tuple-element.20), channel_id=1, source_target_pairs={{1,2},{3,4},{5,6},{7,8},{9,10},{11,12},{13,14},{15,16},{17,18},{19... | collective-permute-start | bytes 393224 | tf_op jit(solution)/shard_map/ppermute | solution.py:350
  9.8 7.5 %collective-permute-start.2 = (bf16[128,1024]{1,0:T(8,128)(2,1)S(1)}, bf16[128,1024]{1,0:T(8,128)(2,1)S(1)}, u32[]{:S(2)}, u32[]{:S(2)}) collective-permute-start(bf16[128,1024]{1,0:T(8,128)(2,1)S(1)} %get-tuple-element.13), channel_id=1, source_target_pairs={{0,32},{64,96},{32,0},{96,64},{1,33},{65,97},{33,1},{97,65},{2,34}... | collective-permute-start | bytes 786440 | tf_op jit(solution)/shard_map/ppermute | solution.py:350
  10.8 9.2 %collective-permute-start.3 = (bf16[128,1024]{1,0:T(8,128)(2,1)S(1)}, bf16[128,1024]{1,0:T(8,128)(2,1)S(1)}, u32[]{:S(2)}, u32[]{:S(2)}) collective-permute-start(bf16[128,1024]{1,0:T(8,128)(2,1)S(1)} %get-tuple-element.14), channel_id=1, source_target_pairs={{32,64},{64,32},{33,65},{65,33},{34,66},{66,34},{35,67},{67,35},{3... | collective-permute-start | bytes 786440 | tf_op jit(solution)/shard_map/ppermute | solution.py:350
  21.0 31.3 %collective-permute-start.4 = (f32[4,16,1024]{2,1,0:T(8,128)S(1)}, f32[4,16,1024]{2,1,0:T(8,128)S(1)}, u32[]{:S(2)}, u32[]{:S(2)}) collective-permute-start(f32[4,16,1024]{2,1,0:T(8,128)S(1)} %get-tuple-element.16), channel_id=1, source_target_pairs={{0,1},{2,3},{4,5},{6,7},{8,9},{10,11},{12,13},{14,15},{16,17},{18,... | collective-permute-start | bytes 786440 | tf_op jit(solution)/shard_map/ppermute | solution.py:350
  25.6 26.7 %collective-permute-start.5 = (f32[4,16,1024]{2,1,0:T(8,128)S(1)}, f32[4,16,1024]{2,1,0:T(8,128)S(1)}, u32[]{:S(2)}, u32[]{:S(2)}) collective-permute-start(f32[4,16,1024]{2,1,0:T(8,128)S(1)} %get-tuple-element.17), channel_id=1, source_target_pairs={{1,2},{3,4},{5,6},{7,8},{9,10},{11,12},{13,14},{15,16},{17,18},{19... | collective-permute-start | bytes 786440 | tf_op jit(solution)/shard_map/ppermute | solution.py:350

commit v2 on v1

--- a/solution.py
+++ b/solution.py
@@ -159,7 +159,7 @@
     )(half_width, conv_weight, out_cotangent)
 
 
-def beam_kernel(mats_ref, sky_ref, a_ref, b_ref, grad_ref, beam_ref, core_ref, far_ref):
+def beam_kernel(mats_ref, sky_ref, b_ref, a_ref, grad_ref, beam_ref, core_ref, far_ref):
     even = lax.axis_index("sky") % 2 == 0
     f_even = lax.axis_index("freq") % 2 == 0
     row = iota((48, 1024), 0)
@@ -179,14 +179,13 @@
     edges = []
     for f, p in ((0, 0), (3, 5)):
         g = grad_ref[p]
-        high = g.astype(BF16).astype(F32)
-        edges.append(jnp.concatenate([beams[f], high, g - high], axis=0))
+        edges.append(jnp.concatenate([beams[f][:40], g], axis=0))
     core_ref[...] = jnp.where(f_even, edges[1], edges[0]).astype(BF16)
     far_ref[...] = jnp.where(f_even, edges[0], edges[1]).astype(BF16)
 
 
-def beam_of(mats, sky_cube, from_a, from_b, grad):
-    edge = jax.ShapeDtypeStruct((128, 1024), BF16)
+def beam_of(mats, sky_cube, from_b, from_a, grad):
+    edge = jax.ShapeDtypeStruct((80, 1024), BF16)
     return pl.pallas_call(
         beam_kernel,
         out_shape=(jax.ShapeDtypeStruct((4, 48, 1024), BF16), edge, edge),
@@ -195,7 +194,7 @@
         compiler_params=params(),
         cost_estimate=pl.CostEstimate(flops=10**9, bytes_accessed=4 * 2**20, transcendentals=0),
         name="beam",
-    )(mats, sky_cube, from_a, from_b, grad)
+    )(mats, sky_cube, from_b, from_a, grad)
 
 
 def three_shifts(beam):
@@ -208,7 +207,25 @@
     return lax.dot_general(a, b, (((1,), (1,)), ((), ())), preferred_element_type=F32)
 
 
-def inner_kernel(beam_ref, cot_ref, out_ref, shift_ref):
+def pick_taps(gram, step):
+    n = gram.shape[1]
+    col = iota((4, 8, n), 2) % 128
+    diff = col - 40 * (col // 40) - (iota((4, 8, n), 0) * 8 + iota((4, 8, n), 1))
+    tiles = gram.reshape(16, 4, 8, n)
+    parts = [jnp.where((diff == b)[None], tiles, 0.0).sum(axis=1) for b in range(3)]
+    sums = jnp.concatenate(parts, axis=2).reshape(128, 3 * n)
+    top = sums.astype(BF16)
+    rest = sums - top.astype(F32)
+    mid = rest.astype(BF16)
+    low = (rest - mid.astype(F32)).astype(BF16)
+    i = iota((3 * n, 128), 0)
+    b, a, e = i // n, step * (i % n // 128), i % 128 // 40
+    chosen = (iota((3 * n, 128), 1) % 32 == jnp.where(e < 3, 9 * a + 3 * b + e, 99)).astype(F32).astype(BF16)
+    total = dot(top, chosen) + (dot(mid, chosen) + dot(low, chosen))
+    return total.reshape(16, 8, 128).sum(axis=1)
+
+
+def inner_kernel(beam_ref, cot_ref, out_ref, shift_ref, gram_ref):
     for p in range(4):
         shift_ref[pl.ds(128 * p, 128)] = three_shifts(beam_ref[p])
     for f in (1, 0, 2, 3):
@@ -216,51 +233,39 @@
         terms = contract(cot_ref[f].reshape(512, 1024), shift_ref[pl.ds(128 * low, 128 * (high - low))])
         cols = pl.ds(128 * (low - f + 1), 128 * (high - low))
         if f == 1:
-            out_ref[:, cols] = terms
+            gram_ref[:, cols] = terms
         else:
-            out_ref[:, cols] += terms
+            gram_ref[:, cols] += terms
+    out_ref[...] = pick_taps(gram_ref[...], 1)
 
 
 def inner_terms(beam, out_cotangent):
     return pl.pallas_call(
         inner_kernel,
-        out_shape=jax.ShapeDtypeStruct((512, 384), F32),
+        out_shape=jax.ShapeDtypeStruct((16, 128), F32),
         in_specs=[vmem(), vmem()],
         out_specs=vmem(),
-        scratch_shapes=[pltpu.VMEM((512, 1024), BF16)],
+        scratch_shapes=[pltpu.VMEM((512, 1024), BF16), pltpu.VMEM((512, 384), F32)],
         compiler_params=params(),
         cost_estimate=pl.CostEstimate(flops=2 * 10**9, bytes_accessed=6 * 2**20, transcendentals=0),
         name="inner_terms",
     )(beam, out_cotangent)
 
 
-def outer_kernel(gram_ref, core_ref, far_ref, cot_ref, out_ref):
+def outer_kernel(inner_ref, core_ref, far_ref, cot_ref, out_ref):
     even = lax.axis_index("freq") % 2 == 0
-    core, far = core_ref[:48], far_ref[:48]
+    core, far = core_ref[:40], far_ref[:40]
     before = three_shifts(jnp.where(even, far, core))
     after = three_shifts(jnp.where(even, core, far))
-    low = contract(cot_ref[0].reshape(512, 1024), before) + gram_ref[:, :128]
-    high = contract(cot_ref[3].reshape(512, 1024), after) + gram_ref[:, 256:]
-    gram = jnp.concatenate([low, gram_ref[:, 128:256], high], axis=1).reshape(16, 32, 384)
-    col = iota((32, 384), 1) % 128
-    e = col // 40
-    diff = col - 40 * e - iota((32, 384), 0)
-    parts = [jnp.where((diff == b)[None], gram, 0.0).sum(axis=1) for b in range(3)]
-    sums = jnp.concatenate(parts, axis=1)
-    top, rest = split(sums)
-    rest = sums - top.astype(F32)
-    mid = rest.astype(BF16)
-    low_part = (rest - mid.astype(F32)).astype(BF16)
-    n = iota((1152, 128), 0)
-    b, a, e = n // 384, n % 384 // 128, n % 128 // 40
-    chosen = (iota((1152, 128), 1) % 32 == jnp.where(e < 3, 9 * a + 3 * b + e, 99)).astype(F32).astype(BF16)
-    total = dot(top, chosen) + (dot(mid, chosen) + dot(low_part, chosen))
+    low = contract(cot_ref[0].reshape(512, 1024), before)
+    high = contract(cot_ref[3].reshape(512, 1024), after)
+    total = inner_ref[...] + pick_taps(jnp.concatenate([low, high], axis=1), 2)
     placed = jnp.where(iota((16, 128), 1) // 32 == iota((16, 128), 0) % 4, total, 0.0)
     packed = placed.reshape(4, 4, 128).sum(axis=1)
     out_ref[...] = jnp.broadcast_to(packed[None], out_ref.shape)
 
 
-def outer_terms(gram, from_core, from_far, out_cotangent, copies):
+def outer_terms(inner, from_core, from_far, out_cotangent, copies):
     return pl.pallas_call(
         outer_kernel,
         out_shape=jax.ShapeDtypeStruct((copies, 4, 128), F32),
@@ -269,14 +274,14 @@
         compiler_params=params(),
         cost_estimate=pl.CostEstimate(flops=5 * 10**8, bytes_accessed=3 * 2**20, transcendentals=0),
         name="outer_terms",
-    )(gram, from_core, from_far, out_cotangent)
+    )(inner, from_core, from_far, out_cotangent)
 
 
 def spread_kernel(mats_ref, grad_ref, core_ref, far_ref, own_ref, to_a_ref, to_b_ref):
     s_even = lax.axis_index("sky") % 2 == 0
     even = lax.axis_index("freq") % 2 == 0
-    core = core_ref[48:88].astype(F32) + core_ref[88:].astype(F32)
-    far = far_ref[48:88].astype(F32) + far_ref[88:].astype(F32)
+    core = core_ref[40:].astype(F32)
+    far = far_ref[40:].astype(F32)
     row = iota((40, 1024), 0)
     first = jnp.where(lax.axis_index("sky") == 0, 1, 0)
     last = jnp.where(lax.axis_index("sky") == lax.axis_size("sky") - 1, 33, 34)
@@ -361,13 +366,13 @@
     sky_a = pair_swap(jnp.where(s_even, high_rows, low_rows), "sky", False)
     sky_b = pair_swap(jnp.where(s_even, low_rows, high_rows), "sky", True)
     grad, mats, held = back_project(half_width, conv_weight, out_cotangent)
-    beam, to_core, to_far = beam_of(mats, sky_cube, sky_a, sky_b, grad)
+    beam, to_core, to_far = beam_of(mats, sky_cube, sky_b, sky_a, grad)
     from_core, from_far = pair_swap(to_core, "freq", False), pair_swap(to_far, "freq", True)
-    gram = inner_terms(beam, held)
+    inner = inner_terms(beam, held)
     own, to_a, to_b = spread(mats, grad, from_core, from_far)
     row_a, row_b = pair_swap(to_a, "sky", False), pair_swap(to_b, "sky", True)
     copies = lax.axis_size("freq") * lax.axis_size("sky")
-    terms = outer_terms(gram, from_core, from_far, held, copies)
+    terms = outer_terms(inner, from_core, from_far, held, copies)
     gathered = lax.all_to_all(terms, ("freq", "sky"), 0, 0)
     cell_count = freq_count * lax.axis_size("freq") * row_count * lax.axis_size("sky") * length
     return finish(1.0 / math.sqrt(cell_count), own, row_a, row_b, gathered)

time: 53.6 us -> 51.7 us (0.965)
  waiting for transfers between devices: 2.73 us -> 0.13 us
  Pallas kernels: 10.8 us -> 11.7 us
    ppermute x6, waiting for transfers between devices: 2.73 us -> 0.13 us  [pair_swap(): return lax.ppermute(x, axis, pairs + [(j, i) for i, j in pairs])]
    pallas_call x1, Pallas kernels: 1.89 us -> 3.45 us  [inner_terms(): pl.pallas_call(inner_kernel, out_shape=jax.ShapeDtypeStruct((16, 128), F3...]
    pallas_call x1, Pallas kernels: 2.05 us -> 1.35 us  [outer_terms(): pl.pallas_call(outer_kernel, out_shape=jax.ShapeDtypeStruct((copies, 4, 1...]
  transfers between devices with their start and end apart: 6 -> 6, of which waited for: 1 -> 1; matrix products, arithmetic and copies ran while one was open for 0% -> 0% of each run, Pallas kernels for 14% -> 17%
where the time goes in v2:
time: 51.7 us; the launch traced here: 51.5 us
  blocking collectives  23.8 us (46%)
  starting transfers between devices  14.1 us (27%)
  Pallas kernels  11.7 us (23%)
  other arithmetic  1 us (2%)
  between operations  0.74 us (1%)
    all_to_all x1, blocking collectives, per_device(): gathered = lax.all_to_all(terms, ('freq', 'sky'), 0, 0)  23.8 us
    ppermute x6, starting transfers between devices, pair_swap(): return lax.ppermute(x, axis, pairs + [(j, i) for i, j in pairs])  14.1 us
    pallas_call x1, Pallas kernels, back_project(): pl.pallas_call(back_kernel, out_shape=(jax.ShapeDtypeStruct((6, 40, 1024)...  3.78 us
    pallas_call x1, Pallas kernels, inner_terms(): pl.pallas_call(inner_kernel, out_shape=jax.ShapeDtypeStruct((16, 128), F3...  3.45 us
    pallas_call x1, Pallas kernels, outer_terms(): pl.pallas_call(outer_kernel, out_shape=jax.ShapeDtypeStruct((copies, 4, 1...  1.35 us
    pallas_call x1, Pallas kernels, spread(): pl.pallas_call(spread_kernel, out_shape=(jax.ShapeDtypeStruct((4, 32, 102...  1.06 us
    pallas_call x1, Pallas kernels, finish(): pl.pallas_call(body, out_shape=(jax.ShapeDtypeStruct((4, 32, 1024), F32),...  1.04 us
  transfers between devices with their start and end apart: 6, of which 1 were waited for; matrix products, arithmetic and copies ran while one was open for 0% of the time, Pallas kernels for 17%

profile of v2, /device:TPU:1, one launch (start us, length us, event | category | flops | bytes accessed | tf_op | source)
XLA Modules:
  0.0 51.5 jit_solution(3240474724319841796)
XLA Ops:
  0.6 1.0 %broadcast_select_fusion = (bf16[4,16,1024]{2,1,0:T(8,128)(2,1)S(1)}, bf16[4,16,1024]{2,1,0:T(8,128)(2,1)S(1)}) fusion(pred[]{:T(512)S(6)} %eq.5, bf16[4,32,1024]{2,1,0:T(8,128)(2,1)} %sky_ref.1), kind=kLoop, calls=%fused_computation | loop fusion | flops 131072 | bytes 524289 | tf_op jit(solution)/shard_map/jit(_where)/select_n | solution.py:366
  1.6 2.5 %collective-permute-start.1 = (bf16[4,16,1024]{2,1,0:T(8,128)(2,1)S(1)}, bf16[4,16,1024]{2,1,0:T(8,128)(2,1)S(1)}, u32[]{:S(2)}, u32[]{:S(2)}) collective-permute-start(bf16[4,16,1024]{2,1,0:T(8,128)(2,1)S(1)} %get-tuple-element.20), channel_id=1, source_target_pairs={{0,1},{2,3},{4,5},{6,7},{8,9},{10,11},{12,13},{14,15},{16,17},{18,... | collective-permute-start | bytes 393224 | tf_op jit(solution)/shard_map/ppermute | solution.py:355
  4.2 0.0 copy-start
  4.2 0.8 %collective-permute-start = (bf16[4,16,1024]{2,1,0:T(8,128)(2,1)S(1)}, bf16[4,16,1024]{2,1,0:T(8,128)(2,1)S(1)}, u32[]{:S(2)}, u32[]{:S(2)}) collective-permute-start(bf16[4,16,1024]{2,1,0:T(8,128)(2,1)S(1)} %get-tuple-element.21), channel_id=1, source_target_pairs={{1,2},{3,4},{5,6},{7,8},{9,10},{11,12},{13,14},{15,16},{17,18},{19... | collective-permute-start | bytes 393224 | tf_op jit(solution)/shard_map/ppermute | solution.py:355
  5.0 3.8 %back_project.1 = (f32[6,40,1024]{2,1,0:T(8,128)S(1)}, bf16[4,1136,256]{2,1,0:T(8,128)(2,1)S(1)}, bf16[4,16,32,1024]{3,2,1,0:T(8,128)(2,1)S(1)}) custom-call(s32[4]{0:T(128)} %width_hbm.1, bf16[16,27]{1,0:T(8,128)(2,1)} %weight_hbm.1, bf16[16,4,32,1024]{3,2,1,0:T(8,128)(2,1)} %cot_ref.1), custom_call_target="tpu_custom_call" | custom-call | flops 3000000000 | bytes 7340032 | tf_op jit(solution)/shard_map/back_project/pallas_call | solution.py:141
  8.8 0.0 collective-permute-done.1.a_ref
  8.8 0.0 collective-permute-done.b_ref
  8.8 0.0 copy-done
  8.8 1.0 %beam.1 = (bf16[4,48,1024]{2,1,0:T(8,128)(2,1)S(1)}, bf16[80,1024]{1,0:T(8,128)(2,1)S(1)}, bf16[80,1024]{1,0:T(8,128)(2,1)S(1)}) custom-call(bf16[4,1136,256]{2,1,0:T(8,128)(2,1)S(1)} %get-tuple-element.11.mats_ref, bf16[4,32,1024]{2,1,0:T(8,128)(2,1)S(1)} %copy-done, bf16[4,16,1024]{2,1,0:T(8,128)(2,1)S(1)} %collective-permute-done.b_ref, ...), custom_call_target="tpu_custom_call" | custom-call | flops 1000000000 | bytes 4194304 | tf_op jit(solution)/shard_map/beam/pallas_call | solution.py:189
  9.8 1.0 %collective-permute-start.2 = (bf16[80,1024]{1,0:T(8,128)(2,1)S(1)}, bf16[80,1024]{1,0:T(8,128)(2,1)S(1)}, u32[]{:S(2)}, u32[]{:S(2)}) collective-permute-start(bf16[80,1024]{1,0:T(8,128)(2,1)S(1)} %get-tuple-element.13), channel_id=1, source_target_pairs={{0,32},{64,96},{32,0},{96,64},{1,33},{65,97},{33,1},{97,65},{2,34}... | collective-permute-start | bytes 491528 | tf_op jit(solution)/shard_map/ppermute | solution.py:355
  10.8 4.5 %collective-permute-start.3 = (bf16[80,1024]{1,0:T(8,128)(2,1)S(1)}, bf16[80,1024]{1,0:T(8,128)(2,1)S(1)}, u32[]{:S(2)}, u32[]{:S(2)}) collective-permute-start(bf16[80,1024]{1,0:T(8,128)(2,1)S(1)} %get-tuple-element.14), channel_id=1, source_target_pairs={{32,64},{64,32},{33,65},{65,33},{34,66},{66,34},{35,67},{67,35},{3... | collective-permute-start | bytes 491528 | tf_op jit(solution)/shard_map/ppermute | solution.py:355
  15.4 3.5 %inner_terms.1.inner_ref = f32[16,128]{1,0:T(8,128)S(1)} custom-call(bf16[4,48,1024]{2,1,0:T(8,128)(2,1)S(1)} %get-tuple-element.18.beam_ref, bf16[4,16,32,1024]{3,2,1,0:T(8,128)(2,1)S(1)} %get-tuple-element.19.cot_ref), custom_call_target="tpu_custom_call" | custom-call | flops 2000000000 | bytes 6291456 | tf_op jit(solution)/shard_map/inner_terms/pallas_call | solution.py:243
  18.8 0.0 collective-permute-done.2.core_ref
  18.8 0.1 collective-permute-done.3.far_ref
  18.9 1.1 %spread.1 = (f32[4,32,1024]{2,1,0:T(8,128)S(1)}, f32[4,16,1024]{2,1,0:T(8,128)S(1)}, f32[4,16,1024]{2,1,0:T(8,128)S(1)}) custom-call(bf16[4,1136,256]{2,1,0:T(8,128)(2,1)S(1)} %get-tuple-element.11.mats_ref, f32[6,40,1024]{2,1,0:T(8,128)S(1)} %get-tuple-element.12.grad_ref, bf16[80,1024]{1,0:T(8,128)(2,1)S(1)} %collective-permute-done.2.core_ref, ...), custom_call_target="tpu_custom_call" | custom-call | flops 1000000000 | bytes 3145728 | tf_op jit(solution)/shard_map/spread/pallas_call | solution.py:311
  20.0 4.6 %collective-permute-start.4 = (f32[4,16,1024]{2,1,0:T(8,128)S(1)}, f32[4,16,1024]{2,1,0:T(8,128)S(1)}, u32[]{:S(2)}, u32[]{:S(2)}) collective-permute-start(f32[4,16,1024]{2,1,0:T(8,128)S(1)} %get-tuple-element.16), channel_id=1, source_target_pairs={{0,1},{2,3},{4,5},{6,7},{8,9},{10,11},{12,13},{14,15},{16,17},{18,... | collective-permute-start | bytes 786440 | tf_op jit(solution)/shard_map/ppermute | solution.py:355
  24.6 0.7 %collective-permute-start.5 = (f32[4,16,1024]{2,1,0:T(8,128)S(1)}, f32[4,16,1024]{2,1,0:T(8,128)S(1)}, u32[]{:S(2)}, u32[]{:S(2)}) collective-permute-start(f32[4,16,1024]{2,1,0:T(8,128)S(1)} %get-tuple-element.17), channel_id=1, source_target_pairs={{1,2},{3,4},{5,6},{7,8},{9,10},{11,12},{13,14},{15,16},{17,18},{19... | collective-permute-start | bytes 786440 | tf_op jit(solution)/shard_map/ppermute | solution.py:355
  25.3 1.3 %outer_terms.1 = f32[128,4,128]{2,1,0:T(4,128)S(1)} custom-call(f32[16,128]{1,0:T(8,128)S(1)} %inner_terms.1.inner_ref, bf16[80,1024]{1,0:T(8,128)(2,1)S(1)} %collective-permute-done.2.core_ref, bf16[80,1024]{1,0:T(8,128)(2,1)S(1)} %collective-permute-done.3.far_ref, bf16[4,16,32,1024]{3,2,1,0:T(8,128)(2,1)S(1)} %get-tuple-element.19.cot_ref), custom_call_target="tpu_custom_call" | custom-call | flops 500000000 | bytes 3145728 | tf_op jit(solution)/shard_map/outer_terms/pallas_call | solution.py:269
  26.6 23.8 %all_to_all.5.refs_3_ = f32[128,4,128]{2,1,0:T(4,128)S(1)} all-to-all(f32[128,4,128]{2,1,0:T(4,128)S(1)} %outer_terms.1), channel_id=1, replica_groups=mesh['freq'=4,'sky'=32] {'freq','sky'}, dimensions={0} | all-to-all | bytes 524288 | tf_op jit(solution)/shard_map/all_to_all | solution.py:376
  50.4 0.0 collective-permute-done.4.refs_1_
  50.4 0.0 collective-permute-done.5.refs_2_
  50.4 1.0 %finish.1 = (f32[4,32,1024]{2,1,0:T(8,128)}, f32[16,27]{1,0:T(8,128)}) custom-call(f32[4,32,1024]{2,1,0:T(8,128)S(1)} %get-tuple-element.15.refs_0_, f32[4,16,1024]{2,1,0:T(8,128)S(1)} %collective-permute-done.4.refs_1_, f32[4,16,1024]{2,1,0:T(8,128)S(1)} %collective-permute-done.5.refs_2_, f32[128,4,128]{2,1,0:T(4,128)S(1)} %all_to_all.5.refs_3_), custom_call_target="tpu_custom_call" | custom-call | flops 1000000 | bytes 2097152 | tf_op jit(solution)/shard_map/finish/pallas_call | solution.py:340
Async XLA Ops:
  1.6 7.1 %collective-permute-start.1 = (bf16[4,16,1024]{2,1,0:T(8,128)(2,1)S(1)}, bf16[4,16,1024]{2,1,0:T(8,128)(2,1)S(1)}, u32[]{:S(2)}, u32[]{:S(2)}) collective-permute-start(bf16[4,16,1024]{2,1,0:T(8,128)(2,1)S(1)} %get-tuple-element.20), channel_id=1, source_target_pairs={{0,1},{2,3},{4,5},{6,7},{8,9},{10,11},{12,13},{14,15},{16,17},{18,... | collective-permute-start | bytes 393224 | tf_op jit(solution)/shard_map/ppermute | solution.py:355
  4.2 4.6 %copy-start = (bf16[4,32,1024]{2,1,0:T(8,128)(2,1)S(1)}, bf16[4,32,1024]{2,1,0:T(8,128)(2,1)}, u32[]{:S(2)}) copy-start(bf16[4,32,1024]{2,1,0:T(8,128)(2,1)} %sky_ref.1) | copy-start | bytes 786436
  4.2 4.6 %collective-permute-start = (bf16[4,16,1024]{2,1,0:T(8,128)(2,1)S(1)}, bf16[4,16,1024]{2,1,0:T(8,128)(2,1)S(1)}, u32[]{:S(2)}, u32[]{:S(2)}) collective-permute-start(bf16[4,16,1024]{2,1,0:T(8,128)(2,1)S(1)} %get-tuple-element.21), channel_id=1, source_target_pairs={{1,2},{3,4},{5,6},{7,8},{9,10},{11,12},{13,14},{15,16},{17,18},{19... | collective-permute-start | bytes 393224 | tf_op jit(solution)/shard_map/ppermute | solution.py:355
  9.8 9.0 %collective-permute-start.2 = (bf16[80,1024]{1,0:T(8,128)(2,1)S(1)}, bf16[80,1024]{1,0:T(8,128)(2,1)S(1)}, u32[]{:S(2)}, u32[]{:S(2)}) collective-permute-start(bf16[80,1024]{1,0:T(8,128)(2,1)S(1)} %get-tuple-element.13), channel_id=1, source_target_pairs={{0,32},{64,96},{32,0},{96,64},{1,33},{65,97},{33,1},{97,65},{2,34}... | collective-permute-start | bytes 491528 | tf_op jit(solution)/shard_map/ppermute | solution.py:355
  10.8 8.1 %collective-permute-start.3 = (bf16[80,1024]{1,0:T(8,128)(2,1)S(1)}, bf16[80,1024]{1,0:T(8,128)(2,1)S(1)}, u32[]{:S(2)}, u32[]{:S(2)}) collective-permute-start(bf16[80,1024]{1,0:T(8,128)(2,1)S(1)} %get-tuple-element.14), channel_id=1, source_target_pairs={{32,64},{64,32},{33,65},{65,33},{34,66},{66,34},{35,67},{67,35},{3... | collective-permute-start | bytes 491528 | tf_op jit(solution)/shard_map/ppermute | solution.py:355
  20.0 30.4 %collective-permute-start.4 = (f32[4,16,1024]{2,1,0:T(8,128)S(1)}, f32[4,16,1024]{2,1,0:T(8,128)S(1)}, u32[]{:S(2)}, u32[]{:S(2)}) collective-permute-start(f32[4,16,1024]{2,1,0:T(8,128)S(1)} %get-tuple-element.16), channel_id=1, source_target_pairs={{0,1},{2,3},{4,5},{6,7},{8,9},{10,11},{12,13},{14,15},{16,17},{18,... | collective-permute-start | bytes 786440 | tf_op jit(solution)/shard_map/ppermute | solution.py:355
  24.6 25.9 %collective-permute-start.5 = (f32[4,16,1024]{2,1,0:T(8,128)S(1)}, f32[4,16,1024]{2,1,0:T(8,128)S(1)}, u32[]{:S(2)}, u32[]{:S(2)}) collective-permute-start(f32[4,16,1024]{2,1,0:T(8,128)S(1)} %get-tuple-element.17), channel_id=1, source_target_pairs={{1,2},{3,4},{5,6},{7,8},{9,10},{11,12},{13,14},{15,16},{17,18},{19... | collective-permute-start | bytes 786440 | tf_op jit(solution)/shard_map/ppermute | solution.py:355

commit v3 on v2

--- a/solution.py
+++ b/solution.py
@@ -302,12 +302,12 @@
     for f in range(4):
         out = dot(mats_ref[f, 1072:, :120], smooth[f])
         own_ref[f] = out[16:48]
-        to_a_ref[f] = jnp.where(s_even, out[48:], out[:16])
-        to_b_ref[f] = jnp.where(s_even, out[:16], out[48:])
+        to_a_ref[f] = jnp.where(s_even, out[48:], out[:16]).astype(BF16)
+        to_b_ref[f] = jnp.where(s_even, out[:16], out[48:]).astype(BF16)
 
 
 def spread(mats, grad, from_core, from_far):
-    edge = jax.ShapeDtypeStruct((4, HALF, 1024), F32)
+    edge = jax.ShapeDtypeStruct((4, HALF, 1024), BF16)
     return pl.pallas_call(
         spread_kernel,
         out_shape=(jax.ShapeDtypeStruct((4, 32, 1024), F32), edge, edge),
@@ -323,8 +323,8 @@
     even = lax.axis_index("sky") % 2 == 0
     for f in range(4):
         ra, rb = a_ref[f], b_ref[f]
-        sky_ref[f, :HALF] = own_ref[f, :HALF] + jnp.where(even, rb, ra)
-        sky_ref[f, HALF:] = own_ref[f, HALF:] + jnp.where(even, ra, rb)
+        sky_ref[f, :HALF] = own_ref[f, :HALF] + jnp.where(even, rb, ra).astype(F32)
+        sky_ref[f, HALF:] = own_ref[f, HALF:] + jnp.where(even, ra, rb).astype(F32)
     packed = jnp.sum(terms_ref[...], axis=0) * scale
     rows = jnp.broadcast_to(packed[:, None, :], (4, 4, 128)).reshape(16, 128)
     placed = jnp.where(iota((16, 128), 1) // 32 == iota((16, 128), 0) % 4, rows, 0.0)
@@ -362,18 +362,21 @@
         pltpu.with_memory_space_constraint(x, pltpu.HBM) for x in (out_cotangent, conv_weight, half_width)
     )
 
-    low_rows, high_rows = sky_cube[:, :HALF], sky_cube[:, HALF:]
-    sky_a = pair_swap(jnp.where(s_even, high_rows, low_rows), "sky", False)
-    sky_b = pair_swap(jnp.where(s_even, low_rows, high_rows), "sky", True)
+    half = lax.axis_index("sky") % 2
+    for_a = lax.dynamic_slice_in_dim(sky_cube, HALF - HALF * half, HALF, 1)
+    for_b = lax.dynamic_slice_in_dim(sky_cube, HALF * half, HALF, 1)
+    sky_a, sky_b = pair_swap(for_a, "sky", False), pair_swap(for_b, "sky", True)
     grad, mats, held = back_project(half_width, conv_weight, out_cotangent)
     beam, to_core, to_far = beam_of(mats, sky_cube, sky_b, sky_a, grad)
     from_core, from_far = pair_swap(to_core, "freq", False), pair_swap(to_far, "freq", True)
     inner = inner_terms(beam, held)
     own, to_a, to_b = spread(mats, grad, from_core, from_far)
-    row_a, row_b = pair_swap(to_a, "sky", False), pair_swap(to_b, "sky", True)
+    own, to_a, to_b, inner = lax.optimization_barrier((own, to_a, to_b, inner))
     copies = lax.axis_size("freq") * lax.axis_size("sky")
     terms = outer_terms(inner, from_core, from_far, held, copies)
+    to_a, to_b, terms = lax.optimization_barrier((to_a, to_b, terms))
     gathered = lax.all_to_all(terms, ("freq", "sky"), 0, 0)
+    row_a, row_b = pair_swap(to_a, "sky", False), pair_swap(to_b, "sky", True)
     cell_count = freq_count * lax.axis_size("freq") * row_count * lax.axis_size("sky") * length
     return finish(1.0 / math.sqrt(cell_count), own, row_a, row_b, gathered)
 

time: 51.7 us -> 50.4 us (0.975)
  the two profiles are of different devices: /device:TPU:1 before, /device:TPU:2 now
where the time goes in v3:
time: 50.4 us; the launch traced here: 50.2 us
  starting transfers between devices  30.7 us (61%)
  Pallas kernels  12.4 us (25%)
  waiting for transfers between devices  5.31 us (11%)
  local copies, waits for them, and re-layouts  1 us (2%)
  between operations  0.75 us (1%)
    ppermute x6, starting transfers between devices, pair_swap(): return lax.ppermute(x, axis, pairs + [(j, i) for i, j in pairs])  17.9 us
    all_to_all x1, starting transfers between devices, per_device(): gathered = lax.all_to_all(terms, ('freq', 'sky'), 0, 0)  12.8 us
    ppermute x6, waiting for transfers between devices, pair_swap(): return lax.ppermute(x, axis, pairs + [(j, i) for i, j in pairs])  5.31 us
    pallas_call x1, Pallas kernels, back_project(): pl.pallas_call(back_kernel, out_shape=(jax.ShapeDtypeStruct((6, 40, 1024)...  3.78 us
    pallas_call x1, Pallas kernels, inner_terms(): pl.pallas_call(inner_kernel, out_shape=jax.ShapeDtypeStruct((16, 128), F3...  3.45 us
    pallas_call x1, Pallas kernels, outer_terms(): pl.pallas_call(outer_kernel, out_shape=jax.ShapeDtypeStruct((copies, 4, 1...  2.06 us
    pallas_call x1, Pallas kernels, spread(): pl.pallas_call(spread_kernel, out_shape=(jax.ShapeDtypeStruct((4, 32, 102...  1.07 us
    pallas_call x1, Pallas kernels, finish(): pl.pallas_call(body, out_shape=(jax.ShapeDtypeStruct((4, 32, 1024), F32),...  1.03 us
  transfers between devices with their start and end apart: 7, of which 2 were waited for; matrix products, arithmetic and copies ran while one was open for 0% of the time, Pallas kernels for 14%

profile of v3, /device:TPU:2, one launch (start us, length us, event | category | flops | bytes accessed | tf_op | source)
XLA Modules:
  0.0 50.2 jit_solution(16856890655802203609)
XLA Ops:
  0.6 1.0 %constant_dynamic-slice_fusion = (bf16[4,16,1024]{2,1,0:T(8,128)(2,1)S(1)}, bf16[4,16,1024]{2,1,0:T(8,128)(2,1)S(1)}) fusion(bf16[4,32,1024]{2,1,0:T(8,128)(2,1)} %sky_ref.1, s32[]{:T(128)S(6)} %select_n.15, s32[]{:T(128)S(6)} %select_n.14), kind=kLoop, calls=%fused_computation | loop fusion | bytes 524296 | tf_op jit(solution)/shard_map/dynamic_slice | solution.py:366
  1.6 2.0 %collective-permute-start.1 = (bf16[4,16,1024]{2,1,0:T(8,128)(2,1)S(1)}, bf16[4,16,1024]{2,1,0:T(8,128)(2,1)S(1)}, u32[]{:S(2)}, u32[]{:S(2)}) collective-permute-start(bf16[4,16,1024]{2,1,0:T(8,128)(2,1)S(1)} %get-tuple-element.34), channel_id=1, source_target_pairs={{0,1},{2,3},{4,5},{6,7},{8,9},{10,11},{12,13},{14,15},{16,17},{18,... | collective-permute-start | bytes 393224 | tf_op jit(solution)/shard_map/ppermute | solution.py:355
  3.6 0.0 copy-start
  3.6 7.0 %collective-permute-start = (bf16[4,16,1024]{2,1,0:T(8,128)(2,1)S(1)}, bf16[4,16,1024]{2,1,0:T(8,128)(2,1)S(1)}, u32[]{:S(2)}, u32[]{:S(2)}) collective-permute-start(bf16[4,16,1024]{2,1,0:T(8,128)(2,1)S(1)} %get-tuple-element.35), channel_id=1, source_target_pairs={{1,2},{3,4},{5,6},{7,8},{9,10},{11,12},{13,14},{15,16},{17,18},{19... | collective-permute-start | bytes 393224 | tf_op jit(solution)/shard_map/ppermute | solution.py:355
  10.6 3.8 %back_project.1 = (f32[6,40,1024]{2,1,0:T(8,128)S(1)}, bf16[4,1136,256]{2,1,0:T(8,128)(2,1)S(1)}, bf16[4,16,32,1024]{3,2,1,0:T(8,128)(2,1)S(1)}) custom-call(s32[4]{0:T(128)} %width_hbm.1, bf16[16,27]{1,0:T(8,128)(2,1)} %weight_hbm.1, bf16[16,4,32,1024]{3,2,1,0:T(8,128)(2,1)} %cot_ref.1), custom_call_target="tpu_custom_call" | custom-call | flops 3000000000 | bytes 7340032 | tf_op jit(solution)/shard_map/back_project/pallas_call | solution.py:141
  14.4 0.0 collective-permute-done.1.a_ref
  14.4 0.4 collective-permute-done.b_ref
  14.8 0.0 copy-done
  14.9 1.0 %beam.1 = (bf16[4,48,1024]{2,1,0:T(8,128)(2,1)S(1)}, bf16[80,1024]{1,0:T(8,128)(2,1)S(1)}, bf16[80,1024]{1,0:T(8,128)(2,1)S(1)}) custom-call(bf16[4,1136,256]{2,1,0:T(8,128)(2,1)S(1)} %get-tuple-element.18.mats_ref, bf16[4,32,1024]{2,1,0:T(8,128)(2,1)S(1)} %copy-done, bf16[4,16,1024]{2,1,0:T(8,128)(2,1)S(1)} %collective-permute-done.b_ref, ...), custom_call_target="tpu_custom_call" | custom-call | flops 1000000000 | bytes 4194304 | tf_op jit(solution)/shard_map/beam/pallas_call | solution.py:189
  15.8 0.1 collective-permute-start.2
  15.9 0.7 %collective-permute-start.3 = (bf16[80,1024]{1,0:T(8,128)(2,1)S(1)}, bf16[80,1024]{1,0:T(8,128)(2,1)S(1)}, u32[]{:S(2)}, u32[]{:S(2)}) collective-permute-start(bf16[80,1024]{1,0:T(8,128)(2,1)S(1)} %get-tuple-element.21), channel_id=1, source_target_pairs={{32,64},{64,32},{33,65},{65,33},{34,66},{66,34},{35,67},{67,35},{3... | collective-permute-start | bytes 491528 | tf_op jit(solution)/shard_map/ppermute | solution.py:355
  16.6 3.4 %inner_terms.1.inner_ref = f32[16,128]{1,0:T(8,128)S(1)} custom-call(bf16[4,48,1024]{2,1,0:T(8,128)(2,1)S(1)} %get-tuple-element.25.beam_ref, bf16[4,16,32,1024]{3,2,1,0:T(8,128)(2,1)S(1)} %get-tuple-element.26.cot_ref), custom_call_target="tpu_custom_call" | custom-call | flops 2000000000 | bytes 6291456 | tf_op jit(solution)/shard_map/inner_terms/pallas_call | solution.py:243
  20.1 0.0 collective-permute-done.2.core_ref
  20.1 0.0 collective-permute-done.3.far_ref
  20.1 1.1 %spread.1 = (f32[4,32,1024]{2,1,0:T(8,128)S(1)}, bf16[4,16,1024]{2,1,0:T(8,128)(2,1)S(1)}, bf16[4,16,1024]{2,1,0:T(8,128)(2,1)S(1)}) custom-call(bf16[4,1136,256]{2,1,0:T(8,128)(2,1)S(1)} %get-tuple-element.18.mats_ref, f32[6,40,1024]{2,1,0:T(8,128)S(1)} %get-tuple-element.19.grad_ref, bf16[80,1024]{1,0:T(8,128)(2,1)S(1)} %collective-permute-done.2.core_ref, ...), custom_call_target="tpu_custom_call" | custom-call | flops 1000000000 | bytes 3145728 | tf_op jit(solution)/shard_map/spread/pallas_call | solution.py:311
  21.1 2.1 %outer_terms.1 = f32[128,4,128]{2,1,0:T(4,128)} custom-call(f32[16,128]{1,0:T(8,128)S(1)} %inner_terms.1.inner_ref, bf16[80,1024]{1,0:T(8,128)(2,1)S(1)} %collective-permute-done.2.core_ref, bf16[80,1024]{1,0:T(8,128)(2,1)S(1)} %collective-permute-done.3.far_ref, bf16[4,16,32,1024]{3,2,1,0:T(8,128)(2,1)S(1)} %get-tuple-element.26.cot_ref), custom_call_target="tpu_custom_call" | custom-call | flops 500000000 | bytes 3145728 | tf_op jit(solution)/shard_map/outer_terms/pallas_call | solution.py:269
  23.2 12.8 %all-to-all-start = ((f32[128,4,128]{2,1,0:T(4,128)}), f32[128,4,128]{2,1,0:T(4,128)S(1)}, u32[]{:S(2)}, u32[]{:S(2)}) async-start(f32[128,4,128]{2,1,0:T(4,128)} %outer_terms.1), calls=%async_computation | async-start | bytes 524288 | tf_op jit(solution)/shard_map/all_to_all | solution.py:378
  36.0 1.7 %collective-permute-start.4 = (bf16[4,16,1024]{2,1,0:T(8,128)(2,1)S(1)}, bf16[4,16,1024]{2,1,0:T(8,128)(2,1)S(1)}, u32[]{:S(2)}, u32[]{:S(2)}) collective-permute-start(bf16[4,16,1024]{2,1,0:T(8,128)(2,1)S(1)} %get-tuple-element.31), channel_id=1, source_target_pairs={{0,1},{2,3},{4,5},{6,7},{8,9},{10,11},{12,13},{14,15},{16,17},{18,... | collective-permute-start | bytes 393224 | tf_op jit(solution)/shard_map/ppermute | solution.py:355
  37.7 6.5 %collective-permute-start.5 = (bf16[4,16,1024]{2,1,0:T(8,128)(2,1)S(1)}, bf16[4,16,1024]{2,1,0:T(8,128)(2,1)S(1)}, u32[]{:S(2)}, u32[]{:S(2)}) collective-permute-start(bf16[4,16,1024]{2,1,0:T(8,128)(2,1)S(1)} %get-tuple-element.32), channel_id=1, source_target_pairs={{1,2},{3,4},{5,6},{7,8},{9,10},{11,12},{13,14},{15,16},{17,18},{19... | collective-permute-start | bytes 393224 | tf_op jit(solution)/shard_map/ppermute | solution.py:355
  44.2 0.0 collective-permute-done.4.refs_1_
  44.3 4.9 %collective-permute-done.5.refs_2_ = bf16[4,16,1024]{2,1,0:T(8,128)(2,1)S(1)} collective-permute-done((bf16[4,16,1024]{2,1,0:T(8,128)(2,1)S(1)}, bf16[4,16,1024]{2,1,0:T(8,128)(2,1)S(1)}, u32[]{:S(2)}, u32[]{:S(2)}) %collective-permute-start.5) | collective-permute-done | bytes 131104 | tf_op jit(solution)/shard_map/ppermute | solution.py:355
  49.1 0.0 all-to-all-done.refs_3_
  49.1 1.0 %finish.1 = (f32[4,32,1024]{2,1,0:T(8,128)}, f32[16,27]{1,0:T(8,128)}) custom-call(f32[4,32,1024]{2,1,0:T(8,128)S(1)} %get-tuple-element.27.refs_0_, bf16[4,16,1024]{2,1,0:T(8,128)(2,1)S(1)} %collective-permute-done.4.refs_1_, bf16[4,16,1024]{2,1,0:T(8,128)(2,1)S(1)} %collective-permute-done.5.refs_2_, f32[128,4,128]{2,1,0:T(4,128)S(1)} %all-to-all-done.refs_3_), custom_call_target="tpu_custom_call" | custom-call | flops 1000000 | bytes 2097152 | tf_op jit(solution)/shard_map/finish/pallas_call | solution.py:340
Async XLA Ops:
  1.6 12.8 %collective-permute-start.1 = (bf16[4,16,1024]{2,1,0:T(8,128)(2,1)S(1)}, bf16[4,16,1024]{2,1,0:T(8,128)(2,1)S(1)}, u32[]{:S(2)}, u32[]{:S(2)}) collective-permute-start(bf16[4,16,1024]{2,1,0:T(8,128)(2,1)S(1)} %get-tuple-element.34), channel_id=1, source_target_pairs={{0,1},{2,3},{4,5},{6,7},{8,9},{10,11},{12,13},{14,15},{16,17},{18,... | collective-permute-start | bytes 393224 | tf_op jit(solution)/shard_map/ppermute | solution.py:355
  3.6 11.2 %copy-start = (bf16[4,32,1024]{2,1,0:T(8,128)(2,1)S(1)}, bf16[4,32,1024]{2,1,0:T(8,128)(2,1)}, u32[]{:S(2)}) copy-start(bf16[4,32,1024]{2,1,0:T(8,128)(2,1)} %sky_ref.1) | copy-start | bytes 786436
  3.6 11.2 %collective-permute-start = (bf16[4,16,1024]{2,1,0:T(8,128)(2,1)S(1)}, bf16[4,16,1024]{2,1,0:T(8,128)(2,1)S(1)}, u32[]{:S(2)}, u32[]{:S(2)}) collective-permute-start(bf16[4,16,1024]{2,1,0:T(8,128)(2,1)S(1)} %get-tuple-element.35), channel_id=1, source_target_pairs={{1,2},{3,4},{5,6},{7,8},{9,10},{11,12},{13,14},{15,16},{17,18},{19... | collective-permute-start | bytes 393224 | tf_op jit(solution)/shard_map/ppermute | solution.py:355
  15.8 4.2 %collective-permute-start.2 = (bf16[80,1024]{1,0:T(8,128)(2,1)S(1)}, bf16[80,1024]{1,0:T(8,128)(2,1)S(1)}, u32[]{:S(2)}, u32[]{:S(2)}) collective-permute-start(bf16[80,1024]{1,0:T(8,128)(2,1)S(1)} %get-tuple-element.20), channel_id=1, source_target_pairs={{0,32},{64,96},{32,0},{96,64},{1,33},{65,97},{33,1},{97,65},{2,34}... | collective-permute-start | bytes 491528 | tf_op jit(solution)/shard_map/ppermute | solution.py:355
  15.9 4.1 %collective-permute-start.3 = (bf16[80,1024]{1,0:T(8,128)(2,1)S(1)}, bf16[80,1024]{1,0:T(8,128)(2,1)S(1)}, u32[]{:S(2)}, u32[]{:S(2)}) collective-permute-start(bf16[80,1024]{1,0:T(8,128)(2,1)S(1)} %get-tuple-element.21), channel_id=1, source_target_pairs={{32,64},{64,32},{33,65},{65,33},{34,66},{66,34},{35,67},{67,35},{3... | collective-permute-start | bytes 491528 | tf_op jit(solution)/shard_map/ppermute | solution.py:355
  23.2 25.9 %all-to-all-start = ((f32[128,4,128]{2,1,0:T(4,128)}), f32[128,4,128]{2,1,0:T(4,128)S(1)}, u32[]{:S(2)}, u32[]{:S(2)}) async-start(f32[128,4,128]{2,1,0:T(4,128)} %outer_terms.1), calls=%async_computation | async-start | bytes 524288 | tf_op jit(solution)/shard_map/all_to_all | solution.py:378
  36.0 8.2 %collective-permute-start.4 = (bf16[4,16,1024]{2,1,0:T(8,128)(2,1)S(1)}, bf16[4,16,1024]{2,1,0:T(8,128)(2,1)S(1)}, u32[]{:S(2)}, u32[]{:S(2)}) collective-permute-start(bf16[4,16,1024]{2,1,0:T(8,128)(2,1)S(1)} %get-tuple-element.31), channel_id=1, source_target_pairs={{0,1},{2,3},{4,5},{6,7},{8,9},{10,11},{12,13},{14,15},{16,17},{18,... | collective-permute-start | bytes 393224 | tf_op jit(solution)/shard_map/ppermute | solution.py:355
  37.7 11.4 %collective-permute-start.5 = (bf16[4,16,1024]{2,1,0:T(8,128)(2,1)S(1)}, bf16[4,16,1024]{2,1,0:T(8,128)(2,1)S(1)}, u32[]{:S(2)}, u32[]{:S(2)}) collective-permute-start(bf16[4,16,1024]{2,1,0:T(8,128)(2,1)S(1)} %get-tuple-element.32), channel_id=1, source_target_pairs={{1,2},{3,4},{5,6},{7,8},{9,10},{11,12},{13,14},{15,16},{17,18},{19... | collective-permute-start | bytes 393224 | tf_op jit(solution)/shard_map/ppermute | solution.py:355

commit v4 on v3

--- a/solution.py
+++ b/solution.py
@@ -265,18 +265,6 @@
     out_ref[...] = jnp.broadcast_to(packed[None], out_ref.shape)
 
 
-def outer_terms(inner, from_core, from_far, out_cotangent, copies):
-    return pl.pallas_call(
-        outer_kernel,
-        out_shape=jax.ShapeDtypeStruct((copies, 4, 128), F32),
-        in_specs=[vmem()] * 4,
-        out_specs=vmem(),
-        compiler_params=params(),
-        cost_estimate=pl.CostEstimate(flops=5 * 10**8, bytes_accessed=3 * 2**20, transcendentals=0),
-        name="outer_terms",
-    )(inner, from_core, from_far, out_cotangent)
-
-
 def spread_kernel(mats_ref, grad_ref, core_ref, far_ref, own_ref, to_a_ref, to_b_ref):
     s_even = lax.axis_index("sky") % 2 == 0
     even = lax.axis_index("freq") % 2 == 0
@@ -306,17 +294,22 @@
         to_b_ref[f] = jnp.where(s_even, out[:16], out[48:]).astype(BF16)
 
 
-def spread(mats, grad, from_core, from_far):
+def spread_and_outer(mats, grad, from_core, from_far, inner, held, copies):
+    def body(mats_ref, grad_ref, core_ref, far_ref, inner_ref, cot_ref, own_ref, to_a_ref, to_b_ref, terms_ref):
+        outer_kernel(inner_ref, core_ref, far_ref, cot_ref, terms_ref)
+        spread_kernel(mats_ref, grad_ref, core_ref, far_ref, own_ref, to_a_ref, to_b_ref)
+
     edge = jax.ShapeDtypeStruct((4, HALF, 1024), BF16)
-    return pl.pallas_call(
-        spread_kernel,
-        out_shape=(jax.ShapeDtypeStruct((4, 32, 1024), F32), edge, edge),
-        in_specs=[vmem()] * 4,
-        out_specs=(vmem(), vmem(), vmem()),
-        compiler_params=params(),
-        cost_estimate=pl.CostEstimate(flops=10**9, bytes_accessed=3 * 2**20, transcendentals=0),
-        name="spread",
-    )(mats, grad, from_core, from_far)
+    terms = jax.ShapeDtypeStruct((copies, 4, 128), F32)
+    return pl.pallas_call(
+        body,
+        out_shape=(jax.ShapeDtypeStruct((4, 32, 1024), F32), edge, edge, terms),
+        in_specs=[vmem()] * 6,
+        out_specs=(vmem(),) * 4,
+        compiler_params=params(),
+        cost_estimate=pl.CostEstimate(flops=15 * 10**8, bytes_accessed=6 * 2**20, transcendentals=0),
+        name="spread_and_outer",
+    )(mats, grad, from_core, from_far, inner, held)
 
 
 def final_kernel(scale, own_ref, a_ref, b_ref, terms_ref, sky_ref, grad_ref):
@@ -370,11 +363,8 @@
     beam, to_core, to_far = beam_of(mats, sky_cube, sky_b, sky_a, grad)
     from_core, from_far = pair_swap(to_core, "freq", False), pair_swap(to_far, "freq", True)
     inner = inner_terms(beam, held)
-    own, to_a, to_b = spread(mats, grad, from_core, from_far)
-    own, to_a, to_b, inner = lax.optimization_barrier((own, to_a, to_b, inner))
     copies = lax.axis_size("freq") * lax.axis_size("sky")
-    terms = outer_terms(inner, from_core, from_far, held, copies)
-    to_a, to_b, terms = lax.optimization_barrier((to_a, to_b, terms))
+    own, to_a, to_b, terms = spread_and_outer(mats, grad, from_core, from_far, inner, held, copies)
     gathered = lax.all_to_all(terms, ("freq", "sky"), 0, 0)
     row_a, row_b = pair_swap(to_a, "sky", False), pair_swap(to_b, "sky", True)
     cell_count = freq_count * lax.axis_size("freq") * row_count * lax.axis_size("sky") * length

time: 50.4 us -> 49.4 us (0.980)
  Pallas kernels: 12.4 us -> 11.4 us
    pallas_call x2 -> x1, Pallas kernels: 3.12 us -> 2.15 us  [spread_and_outer(): pl.pallas_call(body, out_shape=(jax.ShapeDtypeStruct((4, 32, 1024), F32),...]
  transfers between devices with their start and end apart: 7 -> 7, of which waited for: 2 -> 2; matrix products, arithmetic and copies ran while one was open for 0% -> 0% of each run, Pallas kernels for 14% -> 15%
where the time goes in v4:
time: 49.4 us; the launch traced here: 49.2 us
  starting transfers between devices  30.7 us (62%)
  Pallas kernels  11.4 us (23%)
  waiting for transfers between devices  5.31 us (11%)
  local copies, waits for them, and re-layouts  1 us (2%)
  between operations  0.76 us (2%)
    ppermute x6, starting transfers between devices, pair_swap(): return lax.ppermute(x, axis, pairs + [(j, i) for i, j in pairs])  17.9 us
    all_to_all x1, starting transfers between devices, per_device(): gathered = lax.all_to_all(terms, ('freq', 'sky'), 0, 0)  12.8 us
    ppermute x6, waiting for transfers between devices, pair_swap(): return lax.ppermute(x, axis, pairs + [(j, i) for i, j in pairs])  5.31 us
    pallas_call x1, Pallas kernels, back_project(): pl.pallas_call(back_kernel, out_shape=(jax.ShapeDtypeStruct((6, 40, 1024)...  3.78 us
    pallas_call x1, Pallas kernels, inner_terms(): pl.pallas_call(inner_kernel, out_shape=jax.ShapeDtypeStruct((16, 128), F3...  3.45 us
    pallas_call x1, Pallas kernels, spread_and_outer(): pl.pallas_call(body, out_shape=(jax.ShapeDtypeStruct((4, 32, 1024), F32),...  2.15 us
    pallas_call x1, Pallas kernels, finish(): pl.pallas_call(body, out_shape=(jax.ShapeDtypeStruct((4, 32, 1024), F32),...  1.03 us
    dynamic_slice x1, local copies, waits for them, and re-layouts, per_device(): for_a = lax.dynamic_slice_in_dim(sky_cube, HALF - HALF * half, HALF, 1)  1 us
  transfers between devices with their start and end apart: 7, of which 2 were waited for; matrix products, arithmetic and copies ran while one was open for 0% of the time, Pallas kernels for 15%

profile of v4, /device:TPU:2, one launch (start us, length us, event | category | flops | bytes accessed | tf_op | source)
XLA Modules:
  0.0 49.2 jit_solution(11919651860379989303)
XLA Ops:
  0.6 1.0 %constant_dynamic-slice_fusion = (bf16[4,16,1024]{2,1,0:T(8,128)(2,1)S(1)}, bf16[4,16,1024]{2,1,0:T(8,128)(2,1)S(1)}) fusion(bf16[4,32,1024]{2,1,0:T(8,128)(2,1)} %sky_ref.1, s32[]{:T(128)S(6)} %select_n.15, s32[]{:T(128)S(6)} %select_n.14), kind=kLoop, calls=%fused_computation | loop fusion | bytes 524296 | tf_op jit(solution)/shard_map/dynamic_slice | solution.py:359
  1.6 2.0 %collective-permute-start.1 = (bf16[4,16,1024]{2,1,0:T(8,128)(2,1)S(1)}, bf16[4,16,1024]{2,1,0:T(8,128)(2,1)S(1)}, u32[]{:S(2)}, u32[]{:S(2)}) collective-permute-start(bf16[4,16,1024]{2,1,0:T(8,128)(2,1)S(1)} %get-tuple-element.22), channel_id=1, source_target_pairs={{0,1},{2,3},{4,5},{6,7},{8,9},{10,11},{12,13},{14,15},{16,17},{18,... | collective-permute-start | bytes 393224 | tf_op jit(solution)/shard_map/ppermute | solution.py:348
  3.6 0.0 copy-start
  3.6 7.0 %collective-permute-start = (bf16[4,16,1024]{2,1,0:T(8,128)(2,1)S(1)}, bf16[4,16,1024]{2,1,0:T(8,128)(2,1)S(1)}, u32[]{:S(2)}, u32[]{:S(2)}) collective-permute-start(bf16[4,16,1024]{2,1,0:T(8,128)(2,1)S(1)} %get-tuple-element.23), channel_id=1, source_target_pairs={{1,2},{3,4},{5,6},{7,8},{9,10},{11,12},{13,14},{15,16},{17,18},{19... | collective-permute-start | bytes 393224 | tf_op jit(solution)/shard_map/ppermute | solution.py:348
  10.6 3.8 %back_project.1 = (f32[6,40,1024]{2,1,0:T(8,128)S(1)}, bf16[4,1136,256]{2,1,0:T(8,128)(2,1)S(1)}, bf16[4,16,32,1024]{3,2,1,0:T(8,128)(2,1)S(1)}) custom-call(s32[4]{0:T(128)} %width_hbm.1, bf16[16,27]{1,0:T(8,128)(2,1)} %weight_hbm.1, bf16[16,4,32,1024]{3,2,1,0:T(8,128)(2,1)} %cot_ref.1), custom_call_target="tpu_custom_call" | custom-call | flops 3000000000 | bytes 7340032 | tf_op jit(solution)/shard_map/back_project/pallas_call | solution.py:141
  14.4 0.0 collective-permute-done.1.a_ref
  14.4 0.4 collective-permute-done.b_ref
  14.8 0.0 copy-done
  14.9 1.0 %beam.1 = (bf16[4,48,1024]{2,1,0:T(8,128)(2,1)S(1)}, bf16[80,1024]{1,0:T(8,128)(2,1)S(1)}, bf16[80,1024]{1,0:T(8,128)(2,1)S(1)}) custom-call(bf16[4,1136,256]{2,1,0:T(8,128)(2,1)S(1)} %get-tuple-element.12.mats_ref, bf16[4,32,1024]{2,1,0:T(8,128)(2,1)S(1)} %copy-done, bf16[4,16,1024]{2,1,0:T(8,128)(2,1)S(1)} %collective-permute-done.b_ref, ...), custom_call_target="tpu_custom_call" | custom-call | flops 1000000000 | bytes 4194304 | tf_op jit(solution)/shard_map/beam/pallas_call | solution.py:189
  15.8 0.1 collective-permute-start.2
  15.9 0.7 %collective-permute-start.3 = (bf16[80,1024]{1,0:T(8,128)(2,1)S(1)}, bf16[80,1024]{1,0:T(8,128)(2,1)S(1)}, u32[]{:S(2)}, u32[]{:S(2)}) collective-permute-start(bf16[80,1024]{1,0:T(8,128)(2,1)S(1)} %get-tuple-element.15), channel_id=1, source_target_pairs={{32,64},{64,32},{33,65},{65,33},{34,66},{66,34},{35,67},{67,35},{3... | collective-permute-start | bytes 491528 | tf_op jit(solution)/shard_map/ppermute | solution.py:348
  16.6 3.4 %inner_terms.1.inner_ref = f32[16,128]{1,0:T(8,128)S(1)} custom-call(bf16[4,48,1024]{2,1,0:T(8,128)(2,1)S(1)} %get-tuple-element.16.beam_ref, bf16[4,16,32,1024]{3,2,1,0:T(8,128)(2,1)S(1)} %get-tuple-element.17.cot_ref), custom_call_target="tpu_custom_call" | custom-call | flops 2000000000 | bytes 6291456 | tf_op jit(solution)/shard_map/inner_terms/pallas_call | solution.py:243
  20.1 0.0 collective-permute-done.2.core_ref
  20.1 0.0 collective-permute-done.3.far_ref
  20.1 2.2 %spread_and_outer.1 = (f32[4,32,1024]{2,1,0:T(8,128)S(1)}, bf16[4,16,1024]{2,1,0:T(8,128)(2,1)S(1)}, bf16[4,16,1024]{2,1,0:T(8,128)(2,1)S(1)}, f32[128,4,128]{2,1,0:T(4,128)}) custom-call(bf16[4,1136,256]{2,1,0:T(8,128)(2,1)S(1)} %get-tuple-element.12.mats_ref, f32[6,40,1024]{2,1,0:T(8,128)S(1)} %get-tuple-element.13.grad_ref, ...), custom_call_target="tpu_custom_call" | custom-call | flops 1500000000 | bytes 6291456 | tf_op jit(solution)/shard_map/spread_and_outer/pallas_call | solution.py:304
  22.2 12.8 %all-to-all-start = ((f32[128,4,128]{2,1,0:T(4,128)}), f32[128,4,128]{2,1,0:T(4,128)S(1)}, u32[]{:S(2)}, u32[]{:S(2)}) async-start(f32[128,4,128]{2,1,0:T(4,128)} %get-tuple-element.21), calls=%async_computation | async-start | bytes 524288 | tf_op jit(solution)/shard_map/all_to_all | solution.py:368
  35.1 1.7 %collective-permute-start.4 = (bf16[4,16,1024]{2,1,0:T(8,128)(2,1)S(1)}, bf16[4,16,1024]{2,1,0:T(8,128)(2,1)S(1)}, u32[]{:S(2)}, u32[]{:S(2)}) collective-permute-start(bf16[4,16,1024]{2,1,0:T(8,128)(2,1)S(1)} %get-tuple-element.19), channel_id=1, source_target_pairs={{0,1},{2,3},{4,5},{6,7},{8,9},{10,11},{12,13},{14,15},{16,17},{18,... | collective-permute-start | bytes 393224 | tf_op jit(solution)/shard_map/ppermute | solution.py:348
  36.7 6.5 %collective-permute-start.5 = (bf16[4,16,1024]{2,1,0:T(8,128)(2,1)S(1)}, bf16[4,16,1024]{2,1,0:T(8,128)(2,1)S(1)}, u32[]{:S(2)}, u32[]{:S(2)}) collective-permute-start(bf16[4,16,1024]{2,1,0:T(8,128)(2,1)S(1)} %get-tuple-element.20), channel_id=1, source_target_pairs={{1,2},{3,4},{5,6},{7,8},{9,10},{11,12},{13,14},{15,16},{17,18},{19... | collective-permute-start | bytes 393224 | tf_op jit(solution)/shard_map/ppermute | solution.py:348
  43.3 0.0 collective-permute-done.4.refs_1_
  43.3 4.9 %collective-permute-done.5.refs_2_ = bf16[4,16,1024]{2,1,0:T(8,128)(2,1)S(1)} collective-permute-done((bf16[4,16,1024]{2,1,0:T(8,128)(2,1)S(1)}, bf16[4,16,1024]{2,1,0:T(8,128)(2,1)S(1)}, u32[]{:S(2)}, u32[]{:S(2)}) %collective-permute-start.5) | collective-permute-done | bytes 131104 | tf_op jit(solution)/shard_map/ppermute | solution.py:348
  48.2 0.0 all-to-all-done.refs_3_
  48.2 1.0 %finish.1 = (f32[4,32,1024]{2,1,0:T(8,128)}, f32[16,27]{1,0:T(8,128)}) custom-call(f32[4,32,1024]{2,1,0:T(8,128)S(1)} %get-tuple-element.18.refs_0_, bf16[4,16,1024]{2,1,0:T(8,128)(2,1)S(1)} %collective-permute-done.4.refs_1_, bf16[4,16,1024]{2,1,0:T(8,128)(2,1)S(1)} %collective-permute-done.5.refs_2_, f32[128,4,128]{2,1,0:T(4,128)S(1)} %all-to-all-done.refs_3_), custom_call_target="tpu_custom_call" | custom-call | flops 1000000 | bytes 2097152 | tf_op jit(solution)/shard_map/finish/pallas_call | solution.py:333
Async XLA Ops:
  1.6 12.8 %collective-permute-start.1 = (bf16[4,16,1024]{2,1,0:T(8,128)(2,1)S(1)}, bf16[4,16,1024]{2,1,0:T(8,128)(2,1)S(1)}, u32[]{:S(2)}, u32[]{:S(2)}) collective-permute-start(bf16[4,16,1024]{2,1,0:T(8,128)(2,1)S(1)} %get-tuple-element.22), channel_id=1, source_target_pairs={{0,1},{2,3},{4,5},{6,7},{8,9},{10,11},{12,13},{14,15},{16,17},{18,... | collective-permute-start | bytes 393224 | tf_op jit(solution)/shard_map/ppermute | solution.py:348
  3.6 11.2 %copy-start = (bf16[4,32,1024]{2,1,0:T(8,128)(2,1)S(1)}, bf16[4,32,1024]{2,1,0:T(8,128)(2,1)}, u32[]{:S(2)}) copy-start(bf16[4,32,1024]{2,1,0:T(8,128)(2,1)} %sky_ref.1) | copy-start | bytes 786436
  3.6 11.2 %collective-permute-start = (bf16[4,16,1024]{2,1,0:T(8,128)(2,1)S(1)}, bf16[4,16,1024]{2,1,0:T(8,128)(2,1)S(1)}, u32[]{:S(2)}, u32[]{:S(2)}) collective-permute-start(bf16[4,16,1024]{2,1,0:T(8,128)(2,1)S(1)} %get-tuple-element.23), channel_id=1, source_target_pairs={{1,2},{3,4},{5,6},{7,8},{9,10},{11,12},{13,14},{15,16},{17,18},{19... | collective-permute-start | bytes 393224 | tf_op jit(solution)/shard_map/ppermute | solution.py:348
  15.8 4.2 %collective-permute-start.2 = (bf16[80,1024]{1,0:T(8,128)(2,1)S(1)}, bf16[80,1024]{1,0:T(8,128)(2,1)S(1)}, u32[]{:S(2)}, u32[]{:S(2)}) collective-permute-start(bf16[80,1024]{1,0:T(8,128)(2,1)S(1)} %get-tuple-element.14), channel_id=1, source_target_pairs={{0,32},{64,96},{32,0},{96,64},{1,33},{65,97},{33,1},{97,65},{2,34}... | collective-permute-start | bytes 491528 | tf_op jit(solution)/shard_map/ppermute | solution.py:348
  15.9 4.1 %collective-permute-start.3 = (bf16[80,1024]{1,0:T(8,128)(2,1)S(1)}, bf16[80,1024]{1,0:T(8,128)(2,1)S(1)}, u32[]{:S(2)}, u32[]{:S(2)}) collective-permute-start(bf16[80,1024]{1,0:T(8,128)(2,1)S(1)} %get-tuple-element.15), channel_id=1, source_target_pairs={{32,64},{64,32},{33,65},{65,33},{34,66},{66,34},{35,67},{67,35},{3... | collective-permute-start | bytes 491528 | tf_op jit(solution)/shard_map/ppermute | solution.py:348
  22.2 25.9 %all-to-all-start = ((f32[128,4,128]{2,1,0:T(4,128)}), f32[128,4,128]{2,1,0:T(4,128)S(1)}, u32[]{:S(2)}, u32[]{:S(2)}) async-start(f32[128,4,128]{2,1,0:T(4,128)} %get-tuple-element.21), calls=%async_computation | async-start | bytes 524288 | tf_op jit(solution)/shard_map/all_to_all | solution.py:368
  35.1 8.2 %collective-permute-start.4 = (bf16[4,16,1024]{2,1,0:T(8,128)(2,1)S(1)}, bf16[4,16,1024]{2,1,0:T(8,128)(2,1)S(1)}, u32[]{:S(2)}, u32[]{:S(2)}) collective-permute-start(bf16[4,16,1024]{2,1,0:T(8,128)(2,1)S(1)} %get-tuple-element.19), channel_id=1, source_target_pairs={{0,1},{2,3},{4,5},{6,7},{8,9},{10,11},{12,13},{14,15},{16,17},{18,... | collective-permute-start | bytes 393224 | tf_op jit(solution)/shard_map/ppermute | solution.py:348
  36.7 11.4 %collective-permute-start.5 = (bf16[4,16,1024]{2,1,0:T(8,128)(2,1)S(1)}, bf16[4,16,1024]{2,1,0:T(8,128)(2,1)S(1)}, u32[]{:S(2)}, u32[]{:S(2)}) collective-permute-start(bf16[4,16,1024]{2,1,0:T(8,128)(2,1)S(1)} %get-tuple-element.20), channel_id=1, source_target_pairs={{1,2},{3,4},{5,6},{7,8},{9,10},{11,12},{13,14},{15,16},{17,18},{19... | collective-permute-start | bytes 393224 | tf_op jit(solution)/shard_map/ppermute | solution.py:348

commit v5 on v4

--- a/solution.py
+++ b/solution.py
@@ -296,8 +296,8 @@
 
 def spread_and_outer(mats, grad, from_core, from_far, inner, held, copies):
     def body(mats_ref, grad_ref, core_ref, far_ref, inner_ref, cot_ref, own_ref, to_a_ref, to_b_ref, terms_ref):
+        spread_kernel(mats_ref, grad_ref, core_ref, far_ref, own_ref, to_a_ref, to_b_ref)
         outer_kernel(inner_ref, core_ref, far_ref, cot_ref, terms_ref)
-        spread_kernel(mats_ref, grad_ref, core_ref, far_ref, own_ref, to_a_ref, to_b_ref)
 
     edge = jax.ShapeDtypeStruct((4, HALF, 1024), BF16)
     terms = jax.ShapeDtypeStruct((copies, 4, 128), F32)

time: 49.4 us -> 50.2 us (1.016)
  Pallas kernels: 11.4 us -> 12.1 us
    pallas_call x1, Pallas kernels: 2.15 us -> 2.88 us  [spread_and_outer(): pl.pallas_call(body, out_shape=(jax.ShapeDtypeStruct((4, 32, 1024), F32),...]
  transfers between devices with their start and end apart: 7 -> 7, of which waited for: 2 -> 2; matrix products, arithmetic and copies ran while one was open for 0% -> 0% of each run, Pallas kernels for 15% -> 14%
where the time goes in v5:
time: 50.2 us; the launch traced here: 49.9 us
  starting transfers between devices  30.8 us (61%)
  Pallas kernels  12.1 us (24%)
  waiting for transfers between devices  5.31 us (11%)
  local copies, waits for them, and re-layouts  1 us (2%)
  between operations  0.75 us (1%)
    ppermute x6, starting transfers between devices, pair_swap(): return lax.ppermute(x, axis, pairs + [(j, i) for i, j in pairs])  17.9 us
    all_to_all x1, starting transfers between devices, per_device(): gathered = lax.all_to_all(terms, ('freq', 'sky'), 0, 0)  12.8 us
    ppermute x6, waiting for transfers between devices, pair_swap(): return lax.ppermute(x, axis, pairs + [(j, i) for i, j in pairs])  5.31 us
    pallas_call x1, Pallas kernels, back_project(): pl.pallas_call(back_kernel, out_shape=(jax.ShapeDtypeStruct((6, 40, 1024)...  3.78 us
    pallas_call x1, Pallas kernels, inner_terms(): pl.pallas_call(inner_kernel, out_shape=jax.ShapeDtypeStruct((16, 128), F3...  3.45 us
    pallas_call x1, Pallas kernels, spread_and_outer(): pl.pallas_call(body, out_shape=(jax.ShapeDtypeStruct((4, 32, 1024), F32),...  2.88 us
    pallas_call x1, Pallas kernels, finish(): pl.pallas_call(body, out_shape=(jax.ShapeDtypeStruct((4, 32, 1024), F32),...  1.03 us
  transfers between devices with their start and end apart: 7, of which 2 were waited for; matrix products, arithmetic and copies ran while one was open for 0% of the time, Pallas kernels for 14%

profile of v5, /device:TPU:2, one launch (start us, length us, event | category | flops | bytes accessed | tf_op | source)
XLA Modules:
  0.0 49.9 jit_solution(12863738311937903671)
XLA Ops:
  0.6 1.0 %constant_dynamic-slice_fusion = (bf16[4,16,1024]{2,1,0:T(8,128)(2,1)S(1)}, bf16[4,16,1024]{2,1,0:T(8,128)(2,1)S(1)}) fusion(bf16[4,32,1024]{2,1,0:T(8,128)(2,1)} %sky_ref.1, s32[]{:T(128)S(6)} %select_n.15, s32[]{:T(128)S(6)} %select_n.14), kind=kLoop, calls=%fused_computation | loop fusion | bytes 524296 | tf_op jit(solution)/shard_map/dynamic_slice | solution.py:359
  1.6 2.0 %collective-permute-start.1 = (bf16[4,16,1024]{2,1,0:T(8,128)(2,1)S(1)}, bf16[4,16,1024]{2,1,0:T(8,128)(2,1)S(1)}, u32[]{:S(2)}, u32[]{:S(2)}) collective-permute-start(bf16[4,16,1024]{2,1,0:T(8,128)(2,1)S(1)} %get-tuple-element.22), channel_id=1, source_target_pairs={{0,1},{2,3},{4,5},{6,7},{8,9},{10,11},{12,13},{14,15},{16,17},{18,... | collective-permute-start | bytes 393224 | tf_op jit(solution)/shard_map/ppermute | solution.py:348
  3.6 0.0 copy-start
  3.6 7.0 %collective-permute-start = (bf16[4,16,1024]{2,1,0:T(8,128)(2,1)S(1)}, bf16[4,16,1024]{2,1,0:T(8,128)(2,1)S(1)}, u32[]{:S(2)}, u32[]{:S(2)}) collective-permute-start(bf16[4,16,1024]{2,1,0:T(8,128)(2,1)S(1)} %get-tuple-element.23), channel_id=1, source_target_pairs={{1,2},{3,4},{5,6},{7,8},{9,10},{11,12},{13,14},{15,16},{17,18},{19... | collective-permute-start | bytes 393224 | tf_op jit(solution)/shard_map/ppermute | solution.py:348
  10.6 3.8 %back_project.1 = (f32[6,40,1024]{2,1,0:T(8,128)S(1)}, bf16[4,1136,256]{2,1,0:T(8,128)(2,1)S(1)}, bf16[4,16,32,1024]{3,2,1,0:T(8,128)(2,1)S(1)}) custom-call(s32[4]{0:T(128)} %width_hbm.1, bf16[16,27]{1,0:T(8,128)(2,1)} %weight_hbm.1, bf16[16,4,32,1024]{3,2,1,0:T(8,128)(2,1)} %cot_ref.1), custom_call_target="tpu_custom_call" | custom-call | flops 3000000000 | bytes 7340032 | tf_op jit(solution)/shard_map/back_project/pallas_call | solution.py:141
  14.4 0.0 collective-permute-done.1.a_ref
  14.4 0.4 collective-permute-done.b_ref
  14.8 0.0 copy-done
  14.9 1.0 %beam.1 = (bf16[4,48,1024]{2,1,0:T(8,128)(2,1)S(1)}, bf16[80,1024]{1,0:T(8,128)(2,1)S(1)}, bf16[80,1024]{1,0:T(8,128)(2,1)S(1)}) custom-call(bf16[4,1136,256]{2,1,0:T(8,128)(2,1)S(1)} %get-tuple-element.12.mats_ref, bf16[4,32,1024]{2,1,0:T(8,128)(2,1)S(1)} %copy-done, bf16[4,16,1024]{2,1,0:T(8,128)(2,1)S(1)} %collective-permute-done.b_ref, ...), custom_call_target="tpu_custom_call" | custom-call | flops 1000000000 | bytes 4194304 | tf_op jit(solution)/shard_map/beam/pallas_call | solution.py:189
  15.8 0.1 collective-permute-start.2
  15.9 0.7 %collective-permute-start.3 = (bf16[80,1024]{1,0:T(8,128)(2,1)S(1)}, bf16[80,1024]{1,0:T(8,128)(2,1)S(1)}, u32[]{:S(2)}, u32[]{:S(2)}) collective-permute-start(bf16[80,1024]{1,0:T(8,128)(2,1)S(1)} %get-tuple-element.15), channel_id=1, source_target_pairs={{32,64},{64,32},{33,65},{65,33},{34,66},{66,34},{35,67},{67,35},{3... | collective-permute-start | bytes 491528 | tf_op jit(solution)/shard_map/ppermute | solution.py:348
  16.6 3.4 %inner_terms.1.inner_ref = f32[16,128]{1,0:T(8,128)S(1)} custom-call(bf16[4,48,1024]{2,1,0:T(8,128)(2,1)S(1)} %get-tuple-element.16.beam_ref, bf16[4,16,32,1024]{3,2,1,0:T(8,128)(2,1)S(1)} %get-tuple-element.17.cot_ref), custom_call_target="tpu_custom_call" | custom-call | flops 2000000000 | bytes 6291456 | tf_op jit(solution)/shard_map/inner_terms/pallas_call | solution.py:243
  20.1 0.0 collective-permute-done.2.core_ref
  20.1 0.0 collective-permute-done.3.far_ref
  20.1 2.9 %spread_and_outer.1 = (f32[4,32,1024]{2,1,0:T(8,128)S(1)}, bf16[4,16,1024]{2,1,0:T(8,128)(2,1)S(1)}, bf16[4,16,1024]{2,1,0:T(8,128)(2,1)S(1)}, f32[128,4,128]{2,1,0:T(4,128)}) custom-call(bf16[4,1136,256]{2,1,0:T(8,128)(2,1)S(1)} %get-tuple-element.12.mats_ref, f32[6,40,1024]{2,1,0:T(8,128)S(1)} %get-tuple-element.13.grad_ref, ...), custom_call_target="tpu_custom_call" | custom-call | flops 1500000000 | bytes 6291456 | tf_op jit(solution)/shard_map/spread_and_outer/pallas_call | solution.py:304
  23.0 12.8 %all-to-all-start = ((f32[128,4,128]{2,1,0:T(4,128)}), f32[128,4,128]{2,1,0:T(4,128)S(1)}, u32[]{:S(2)}, u32[]{:S(2)}) async-start(f32[128,4,128]{2,1,0:T(4,128)} %get-tuple-element.21), calls=%async_computation | async-start | bytes 524288 | tf_op jit(solution)/shard_map/all_to_all | solution.py:368
  35.8 1.7 %collective-permute-start.4 = (bf16[4,16,1024]{2,1,0:T(8,128)(2,1)S(1)}, bf16[4,16,1024]{2,1,0:T(8,128)(2,1)S(1)}, u32[]{:S(2)}, u32[]{:S(2)}) collective-permute-start(bf16[4,16,1024]{2,1,0:T(8,128)(2,1)S(1)} %get-tuple-element.19), channel_id=1, source_target_pairs={{0,1},{2,3},{4,5},{6,7},{8,9},{10,11},{12,13},{14,15},{16,17},{18,... | collective-permute-start | bytes 393224 | tf_op jit(solution)/shard_map/ppermute | solution.py:348
  37.5 6.5 %collective-permute-start.5 = (bf16[4,16,1024]{2,1,0:T(8,128)(2,1)S(1)}, bf16[4,16,1024]{2,1,0:T(8,128)(2,1)S(1)}, u32[]{:S(2)}, u32[]{:S(2)}) collective-permute-start(bf16[4,16,1024]{2,1,0:T(8,128)(2,1)S(1)} %get-tuple-element.20), channel_id=1, source_target_pairs={{1,2},{3,4},{5,6},{7,8},{9,10},{11,12},{13,14},{15,16},{17,18},{19... | collective-permute-start | bytes 393224 | tf_op jit(solution)/shard_map/ppermute | solution.py:348
  44.0 0.0 collective-permute-done.4.refs_1_
  44.0 4.9 %collective-permute-done.5.refs_2_ = bf16[4,16,1024]{2,1,0:T(8,128)(2,1)S(1)} collective-permute-done((bf16[4,16,1024]{2,1,0:T(8,128)(2,1)S(1)}, bf16[4,16,1024]{2,1,0:T(8,128)(2,1)S(1)}, u32[]{:S(2)}, u32[]{:S(2)}) %collective-permute-start.5) | collective-permute-done | bytes 131104 | tf_op jit(solution)/shard_map/ppermute | solution.py:348
  48.9 0.0 all-to-all-done.refs_3_
  48.9 1.0 %finish.1 = (f32[4,32,1024]{2,1,0:T(8,128)}, f32[16,27]{1,0:T(8,128)}) custom-call(f32[4,32,1024]{2,1,0:T(8,128)S(1)} %get-tuple-element.18.refs_0_, bf16[4,16,1024]{2,1,0:T(8,128)(2,1)S(1)} %collective-permute-done.4.refs_1_, bf16[4,16,1024]{2,1,0:T(8,128)(2,1)S(1)} %collective-permute-done.5.refs_2_, f32[128,4,128]{2,1,0:T(4,128)S(1)} %all-to-all-done.refs_3_), custom_call_target="tpu_custom_call" | custom-call | flops 1000000 | bytes 2097152 | tf_op jit(solution)/shard_map/finish/pallas_call | solution.py:333
Async XLA Ops:
  1.6 12.8 %collective-permute-start.1 = (bf16[4,16,1024]{2,1,0:T(8,128)(2,1)S(1)}, bf16[4,16,1024]{2,1,0:T(8,128)(2,1)S(1)}, u32[]{:S(2)}, u32[]{:S(2)}) collective-permute-start(bf16[4,16,1024]{2,1,0:T(8,128)(2,1)S(1)} %get-tuple-element.22), channel_id=1, source_target_pairs={{0,1},{2,3},{4,5},{6,7},{8,9},{10,11},{12,13},{14,15},{16,17},{18,... | collective-permute-start | bytes 393224 | tf_op jit(solution)/shard_map/ppermute | solution.py:348
  3.6 11.2 %copy-start = (bf16[4,32,1024]{2,1,0:T(8,128)(2,1)S(1)}, bf16[4,32,1024]{2,1,0:T(8,128)(2,1)}, u32[]{:S(2)}) copy-start(bf16[4,32,1024]{2,1,0:T(8,128)(2,1)} %sky_ref.1) | copy-start | bytes 786436
  3.6 11.2 %collective-permute-start = (bf16[4,16,1024]{2,1,0:T(8,128)(2,1)S(1)}, bf16[4,16,1024]{2,1,0:T(8,128)(2,1)S(1)}, u32[]{:S(2)}, u32[]{:S(2)}) collective-permute-start(bf16[4,16,1024]{2,1,0:T(8,128)(2,1)S(1)} %get-tuple-element.23), channel_id=1, source_target_pairs={{1,2},{3,4},{5,6},{7,8},{9,10},{11,12},{13,14},{15,16},{17,18},{19... | collective-permute-start | bytes 393224 | tf_op jit(solution)/shard_map/ppermute | solution.py:348
  15.8 4.2 %collective-permute-start.2 = (bf16[80,1024]{1,0:T(8,128)(2,1)S(1)}, bf16[80,1024]{1,0:T(8,128)(2,1)S(1)}, u32[]{:S(2)}, u32[]{:S(2)}) collective-permute-start(bf16[80,1024]{1,0:T(8,128)(2,1)S(1)} %get-tuple-element.14), channel_id=1, source_target_pairs={{0,32},{64,96},{32,0},{96,64},{1,33},{65,97},{33,1},{97,65},{2,34}... | collective-permute-start | bytes 491528 | tf_op jit(solution)/shard_map/ppermute | solution.py:348
  15.9 4.1 %collective-permute-start.3 = (bf16[80,1024]{1,0:T(8,128)(2,1)S(1)}, bf16[80,1024]{1,0:T(8,128)(2,1)S(1)}, u32[]{:S(2)}, u32[]{:S(2)}) collective-permute-start(bf16[80,1024]{1,0:T(8,128)(2,1)S(1)} %get-tuple-element.15), channel_id=1, source_target_pairs={{32,64},{64,32},{33,65},{65,33},{34,66},{66,34},{35,67},{67,35},{3... | collective-permute-start | bytes 491528 | tf_op jit(solution)/shard_map/ppermute | solution.py:348
  23.0 25.9 %all-to-all-start = ((f32[128,4,128]{2,1,0:T(4,128)}), f32[128,4,128]{2,1,0:T(4,128)S(1)}, u32[]{:S(2)}, u32[]{:S(2)}) async-start(f32[128,4,128]{2,1,0:T(4,128)} %get-tuple-element.21), calls=%async_computation | async-start | bytes 524288 | tf_op jit(solution)/shard_map/all_to_all | solution.py:368
  35.8 8.2 %collective-permute-start.4 = (bf16[4,16,1024]{2,1,0:T(8,128)(2,1)S(1)}, bf16[4,16,1024]{2,1,0:T(8,128)(2,1)S(1)}, u32[]{:S(2)}, u32[]{:S(2)}) collective-permute-start(bf16[4,16,1024]{2,1,0:T(8,128)(2,1)S(1)} %get-tuple-element.19), channel_id=1, source_target_pairs={{0,1},{2,3},{4,5},{6,7},{8,9},{10,11},{12,13},{14,15},{16,17},{18,... | collective-permute-start | bytes 393224 | tf_op jit(solution)/shard_map/ppermute | solution.py:348
  37.5 11.4 %collective-permute-start.5 = (bf16[4,16,1024]{2,1,0:T(8,128)(2,1)S(1)}, bf16[4,16,1024]{2,1,0:T(8,128)(2,1)S(1)}, u32[]{:S(2)}, u32[]{:S(2)}) collective-permute-start(bf16[4,16,1024]{2,1,0:T(8,128)(2,1)S(1)} %get-tuple-element.20), channel_id=1, source_target_pairs={{1,2},{3,4},{5,6},{7,8},{9,10},{11,12},{13,14},{15,16},{17,18},{19... | collective-permute-start | bytes 393224 | tf_op jit(solution)/shard_map/ppermute | solution.py:348
